TPU v7x, 32 devices: a whole 2x2x4 slice. The times are simulated.
32 devices in a mesh: ctx: 8 (over y, x, core), fsdp: 4 (over z).
Axes of the slice: x: 2, y: 2, z: 4, core: 2. Of those that a mesh axis runs over, the one named last changes fastest.
Arguments:
- tokens: bfloat16 [4, 2048, 2048], P('fsdp', 'ctx'), may hold values from -6 to 6
- cotangent: bfloat16 [4, 2048, 2048], P('fsdp', 'ctx'), may hold values from -6 to 6
- doc_starts: int32 [4, 8], P('fsdp'), may hold values from 0 to 2047, as said below
- deal_order: int32 [16], replicated, may hold values from 0 to 15, as said below
- query_key_value_weight: bfloat16 [2048, 1536], P('fsdp'), may hold values from -0.125 to 0.125
- w_out: bfloat16 [1024, 2048], P('fsdp'), may hold values from -1.5 to 1.5
- w_gate: bfloat16 [2048, 1024], P('fsdp'), may hold values from -0.125 to 0.125
- w_up: bfloat16 [2048, 1024], P('fsdp'), may hold values from -0.125 to 0.125
- w_down: bfloat16 [1024, 2048], P('fsdp'), may hold values from -0.1875 to 0.1875
- gain_attn: bfloat16 [2048], P('fsdp'), may hold values from 0.5 to 1.5
- gain_ffn: bfloat16 [2048], P('fsdp'), may hold values from 0.5 to 1.5
- gain_qk: bfloat16 [2, 64], P(None, 'fsdp'), may hold values from 1 to 2
Outputs:
- mixed_out: bfloat16 [4, 2048, 2048], P('fsdp', 'ctx')
- tokens_grad: float32 [4, 2048, 2048], P('fsdp', 'ctx')
- w_qkv_grad: float32 [2048, 1536], P('fsdp')
- w_out_grad: float32 [1024, 2048], P('fsdp')
- w_gate_grad: float32 [2048, 1024], P('fsdp')
- w_up_grad: float32 [2048, 1024], P('fsdp')
- w_down_grad: float32 [1024, 2048], P('fsdp')
- gain_attn_grad: float32 [2048], P('fsdp')
- gain_ffn_grad: float32 [2048], P('fsdp')
- gain_qk_grad: float32 [2, 64], P(None, 'fsdp')
Inputs may be any that keep to these rules, and one draw needn't show every extreme that they name: `doc_starts`: in each pack the first entry is 0 and entries rise; every document (from its start to the next start, the last one to 2048) holds 1 to 1024 tokens, one document of each pack holds exactly 1024, and the last document of each pack holds one token, so its start is 2047. `deal_order`: A permutation of the 16 blocks of a pack; the blocks at stored places 2 c and 2 c + 1 add up to 15.
All inputs are finite; a program needn't handle non-finite values.
Results may differ from a plain program's by a relative error of at most 0.017.
The roundings to bfloat16 on the way count: a program that leaves them out, or rounds other values in their place, can miss the bound.
Values may be sent and summed in bfloat16 or wider, within the bound.
A program may use at most 192 MiB of HBM per device.

v0:
```python
import functools

import jax
import jax.numpy as jnp
from jax import lax
from jax.experimental import pallas as pl
from jax.experimental.pallas import tpu as pltpu
from jax.sharding import PartitionSpec as P

QUERY_HEADS = 16
KEY_VALUE_HEADS = 4
HEAD_SIZE = 64


EPSILON = 1e-06
THETA = 10000.0

MESH = pl.DeviceIdType.MESH
DMA = pltpu.SemaphoreType.DMA
HBM_SPEC = pl.BlockSpec(memory_space=pl.ANY)
VMEM_SPEC = pl.BlockSpec(memory_space=pltpu.VMEM)
SPACING = 2
VMEM_LIMIT = 67043328


def plane_shape(ctx_count):
    chips = ctx_count // 2
    bits = chips.bit_length() - 1
    assert 2**bits == chips and ctx_count == 2 * chips
    return chips, bits


class Place:
    def __init__(self, ctx_count, fsdp_count):
        self.chips, self.bits = plane_shape(ctx_count)
        self.fsdp_count = fsdp_count
        self.ctx = lax.axis_index("ctx")
        self.z = lax.axis_index("fsdp")
        self.core = self.ctx % 2
        chip = self.ctx // 2
        self.bit = [(chip // 2**j) % 2 for j in range(self.bits)]
        self.across = [self.ctx + (1 - 2 * self.bit[j]) * 2 * 2**j for j in range(self.bits)]
        self.partner = self.ctx + 1 - 2 * self.core
        self.orders = (list(range(self.bits)), list(reversed(range(self.bits))))

    def at(self, free=(), other=None):
        return tuple(
            slice(None) if j in free else (1 - self.bit[j] if j == other else self.bit[j])
            for j in reversed(range(self.bits))
        )

    def barrier(self, plane=True, line=True, near=False):
        sem = pltpu.get_barrier_semaphore()
        count = 0
        if plane:
            for p in self.across + [self.partner]:
                pl.semaphore_signal(sem, inc=1, device_id={"ctx": p}, device_id_type=MESH)
                count += 1
        if line:
            for k in range(1, self.fsdp_count):
                pl.semaphore_signal(
                    sem,
                    inc=1,
                    device_id={"fsdp": (self.z + k) % self.fsdp_count},
                    device_id_type=MESH,
                )
                count += 1
        pl.semaphore_wait(sem, count)


def remote(src, dst, send, recv, **where):
    return pltpu.make_async_remote_copy(
        src, dst, send, recv, device_id=where, device_id_type=MESH
    )


def run_ticks(jobs, spacing=SPACING):
    depth = max(len(job) for job in jobs)
    for tick in range(len(jobs) + spacing * (depth - 1)):
        for j in reversed(range(depth)):
            t = tick - spacing * j
            if 0 <= t < len(jobs) and j < len(jobs[t]):
                jobs[t][j]()


def column_half(ref, half):
    n = ref.shape[-1] // 2
    return pl.ds(half * n, n)


def gather_kernel(nf, nc, count, *refs):
    shards, small = refs[:count], refs[count]
    outs, small_out = refs[count + 1 : 2 * count + 1], refs[2 * count + 1]
    stages = refs[2 * count + 2 : 3 * count + 3]
    up_s, up_r, down_s, down_r, ps, pr, cs, cr, ss, sr, load_sem, store_sem = refs[3 * count + 3 :]
    me = Place(nc, nf)
    z = me.z
    loads = [
        pltpu.make_async_copy(src, dst, load_sem.at[i])
        for i, (src, dst) in enumerate(zip(list(shards) + [small], stages))
    ]
    stores = [
        pltpu.make_async_copy(stages[i], dst.at[z], store_sem.at[i])
        for i, dst in enumerate(list(outs) + [small_out])
    ]
    for load in loads:
        load.start()
    me.barrier()

    def source(k):
        pairs = jnp.minimum(z, nf - 1 - z)
        near = (k + 1) // 2
        near_source = z - near if k % 2 == 1 else z + near
        far = k - pairs
        far_source = jnp.where(2 * z < nf - 1, z + far, z - far)
        return jnp.where(k <= 2 * pairs, near_source, far_source)

    sources = [None] + [source(k) for k in range(1, nf)]

    def line_copy(i, src_z, src, up):
        to = z + 1 if up else z - 1
        sems = (up_s, up_r) if up else (down_s, down_r)
        return remote(
            src,
            outs[i].at[(src_z, me.core) + me.at()],
            sems[0].at[i, src_z],
            sems[1].at[i, src_z],
            fsdp=to,
        )

    def line_start(i, src_z, src, up, condition):
        @pl.when(condition)
        def _():
            line_copy(i, src_z, src, up).start()

    def small_copy(k):
        return remote(small, small_out.at[z], ss.at[k], sr.at[k], fsdp=(z + k) % nf)

    for k in range(1, nf):
        small_copy(k).start()
    for i in range(count):
        mine = shards[i].at[(me.core,) + me.at()]
        line_start(i, z, mine, True, z + 1 < nf)
        line_start(i, z, mine, False, z > 0)

    def line_stage(i, k):
        src_z = sources[k]
        here = outs[i].at[(src_z, me.core) + me.at()]
        below = src_z < z

        @pl.when(below)
        def _():
            line_copy(i, src_z, here, True).wait_recv()

        @pl.when(jnp.logical_not(below))
        def _():
            line_copy(i, src_z, here, False).wait_recv()

        line_start(i, src_z, here, True, jnp.logical_and(below, z + 1 < nf))
        line_start(i, src_z, here, False, jnp.logical_and(src_z > z, z > 0))

    def plane_copy(i, k, half, j):
        order = me.orders[half]
        ref = outs[i].at[
            (sources[k], me.core) + me.at(order[:j]) + (slice(None), column_half(outs[i], half))
        ]
        return remote(
            ref, ref, ps.at[half, i, k, j], pr.at[half, i, k, j], ctx=me.across[order[j]]
        )

    def core_copy(i, k):
        ref = outs[i].at[sources[k], me.core]
        return remote(ref, ref, cs.at[i, k], cr.at[i, k], ctx=me.partner)

    def plane_stage(i, k, j):
        if j == 0:
            line_stage(i, k)
        else:
            for half in (0, 1):
                plane_copy(i, k, half, j - 1).wait_recv()
        if j < me.bits:
            for half in (0, 1):
                plane_copy(i, k, half, j).start()
        else:
            core_copy(i, k).start()

    order = [(i, k) for i in range(count) for k in range(1, nf)]
    jobs = [
        [functools.partial(plane_stage, i, k, j) for j in range(me.bits + 1)]
        + [core_copy(i, k).wait_recv]
        for i, k in order
    ]
    for load, store in zip(loads, stores):
        load.wait()
        store.start()
    run_ticks(jobs)
    for k in range(1, nf):
        small_copy(k).wait_recv()
        small_copy(k).wait_send()
    for i in range(count):
        @pl.when(z + 1 < nf)
        def _():
            line_copy(i, z, shards[i].at[(me.core,) + me.at()], True).wait_send()

        @pl.when(z > 0)
        def _():
            line_copy(i, z, shards[i].at[(me.core,) + me.at()], False).wait_send()

    for i, k in order:
        src_z = sources[k]
        here = outs[i].at[(src_z, me.core) + me.at()]

        @pl.when(jnp.logical_and(src_z < z, z + 1 < nf))
        def _():
            line_copy(i, src_z, here, True).wait_send()

        @pl.when(jnp.logical_and(src_z > z, z > 0))
        def _():
            line_copy(i, src_z, here, False).wait_send()

        for half in (0, 1):
            for j in range(me.bits):
                plane_copy(i, k, half, j).wait_send()
        core_copy(i, k).wait_send()
    for store in stores:
        store.wait()


def gather_weights(nf, nc, shards, small):
    _, bits = plane_shape(nc)
    count = len(shards)
    views = [w.reshape((2,) * (1 + bits) + (w.shape[0] // nc, w.shape[1])) for w in shards]
    arrays = views + [small]
    outs = pl.pallas_call(
        functools.partial(gather_kernel, nf, nc, count),
        out_shape=[jax.ShapeDtypeStruct((nf,) + v.shape, v.dtype) for v in arrays],
        in_specs=[HBM_SPEC] * (count + 1),
        out_specs=[HBM_SPEC] * (count + 1),
        scratch_shapes=[pltpu.VMEM(v.shape, v.dtype) for v in arrays]
        + [DMA((count, nf))] * 4
        + [DMA((2, count, nf, bits))] * 2
        + [DMA((count, nf))] * 2
        + [DMA((nf,))] * 2
        + [DMA((count + 1,))] * 2,
        compiler_params=pltpu.CompilerParams(collective_id=0, has_side_effects=True),
        name="gather_weights",
    )(*arrays)
    return [o.reshape(nf * w.shape[0], w.shape[1]) for o, w in zip(outs, shards)], outs[count]


def gather_pair_kernel(nf, nc, pair, out, stage, ps, pr, cs, cr, load_sem, store_sem):
    me = Place(nc, nf)
    load = pltpu.make_async_copy(pair, stage, load_sem)
    load.start()
    me.barrier(line=False)

    def plane_copy(half, j):
        order = me.orders[half]
        where = (slice(None), column_half(out, half))
        dst = out.at[me.at(order[:j]) + (me.core,) + where]
        src = pair.at[where] if j == 0 else dst
        return remote(src, dst, ps.at[half, j], pr.at[half, j], ctx=me.across[order[j]])

    own_core = remote(pair, out.at[me.at() + (me.core,)], cs.at[0, 0], cr.at[0, 0], ctx=me.partner)

    def core_copy(half, j):
        order = me.orders[half]
        ref = out.at[
            me.at(order[:j], other=order[j]) + (me.core, slice(None), column_half(out, half))
        ]
        return remote(ref, ref, cs.at[half, j + 1], cr.at[half, j + 1], ctx=me.partner)

    for half in (0, 1):
        plane_copy(half, 0).start()
    own_core.start()
    load.wait()
    store = pltpu.make_async_copy(stage, out.at[me.at() + (me.core,)], store_sem)
    store.start()
    store.wait()
    for j in range(me.bits):
        for half in (0, 1):
            plane_copy(half, j).wait_recv()
        if j + 1 < me.bits:
            for half in (0, 1):
                plane_copy(half, j + 1).start()
        for half in (0, 1):
            core_copy(half, j).start()
    own_core.wait()
    for j in range(me.bits):
        for half in (0, 1):
            plane_copy(half, j).wait_send()
            core_copy(half, j).wait()


def gather_pair(nf, nc, pair):
    _, bits = plane_shape(nc)
    out = pl.pallas_call(
        functools.partial(gather_pair_kernel, nf, nc),
        out_shape=jax.ShapeDtypeStruct((2,) * (bits + 1) + pair.shape, pair.dtype),
        in_specs=[HBM_SPEC],
        out_specs=HBM_SPEC,
        scratch_shapes=[pltpu.VMEM(pair.shape, pair.dtype)]
        + [DMA((2, bits))] * 2
        + [DMA((2, bits + 1))] * 2
        + [DMA, DMA],
        compiler_params=pltpu.CompilerParams(collective_id=1, has_side_effects=True),
        name="gather_pair",
    )(pair)
    return out.reshape(nc * pair.shape[0], pair.shape[1])


def reduce_kernel(nf, nc, pairs, lefts_count, rights_count, *refs):
    _, bits = plane_shape(nc)
    count = len(pairs)
    rest = list(refs)

    def take(n):
        return [rest.pop(0) for _ in range(n)]

    lefts, rights = take(lefts_count), take(rights_count)
    grad_pair, back_in = take(1)[0], take(BACK_LOADS)
    gain, qk_gain, cosines, sines, ffn_gain_part = take(5)
    outs, (tokens_grad, small_out) = take(count), take(2)
    left_v, right_v, held = take(lefts_count), take(rights_count + 1), take(count)
    ins = [[take(2) for _ in range(bits)] for _ in range(count)]
    line_in, final = take(count), take(count)
    small_sum, small_in, small_line = take(3)
    pair_held, pair_core, *pair_in = take(2 + 2 * bits)
    back_v, grads = take(BACK_LOADS), take(1)[0]
    back_sem, grad_sem, pl_sem, pcs, pcr, pps, ppr = take(7)
    (ll, lls, llr, rl, rls, rlr, ps, pr, ls, lr, gs, gr, cs, cr, own_sem, ss, sr, sls, slr) = rest
    me = Place(nc, nf)
    z = me.z
    rows = rights[0].shape[0]
    projected_v = right_v[rights_count]
    back_loads = [
        pltpu.make_async_copy(src, dst, back_sem.at[n])
        for n, (src, dst) in enumerate(zip(back_in, back_v))
    ]
    every = tuple(slice(None) for _ in range(bits))
    pair_load = pltpu.make_async_copy(grad_pair.at[every + (me.core,)], pair_held, pl_sem)
    pair_core_copy = remote(
        grad_pair.at[every + (1 - me.core,)], pair_core, pcs, pcr, ctx=me.partner
    )

    def left_load(a):
        return pltpu.make_async_copy(
            lefts[a].at[:, me.core], left_v[a].at[:, :, pl.ds(0, rows)], ll.at[a]
        )

    def right_load(b):
        return pltpu.make_async_copy(rights[b], right_v[b].at[pl.ds(0, rows)], rl.at[b])

    def left_copy(a):
        return remote(
            lefts[a].at[:, 1 - me.core],
            left_v[a].at[:, :, pl.ds(rows, rows)],
            lls.at[a],
            llr.at[a],
            ctx=me.partner,
        )

    def right_copy(b):
        src = rights[b] if b < rights_count else projected_v.at[pl.ds(0, rows)]
        return remote(
            src, right_v[b].at[pl.ds(rows, rows)], rls.at[b], rlr.at[b], ctx=me.partner
        )

    order, seen = [], set()
    for a, b in pairs:
        for key in (("left", a), ("right", b)):
            if key not in seen and key != ("right", rights_count):
                seen.add(key)
                order.append(key)
    for at, (side, n) in enumerate(order):
        (left_load if side == "left" else right_load)(n).start()
        if at == 1:
            pair_load.start()
    for load in back_loads:
        load.start()
    me.barrier()
    for at, (side, n) in enumerate(order):
        (left_copy if side == "left" else right_copy)(n).start()
        if at == 1:
            pair_core_copy.start()
    arrived = set()

    def arrive(side, n):
        if (side, n) not in arrived:
            arrived.add((side, n))
            if (side, n) in order:
                (left_load if side == "left" else right_load)(n).wait()
            (left_copy if side == "left" else right_copy)(n).wait_recv()

    def target(k):
        return (z + k) % nf

    def form(i, k):
        a, b = pairs[i]
        arrive("left", a)
        arrive("right", b)
        width = held[i].shape[-1]
        chunk = min(width, CHUNK)

        def body(t, carry):
            cols = pl.ds(pl.multiple_of(t * chunk, chunk), chunk)
            value = dot_plain(left_v[a][target(k)], right_v[b][:, cols]).astype(jnp.bfloat16)
            held[i][target(k), ..., cols] = value.reshape(held[i].shape[1:-1] + (chunk,))
            return carry

        lax.fori_loop(0, width // chunk, body, 0)

    def plane_copy(i, k, half, j):
        order = me.orders[half]
        src = held[i].at[
            (target(k),)
            + me.at(order[j + 1 :], other=order[j])
            + (slice(None), column_half(held[i], half))
        ]
        return remote(
            src,
            ins[i][j][half].at[k],
            ps.at[half, i, k, j],
            pr.at[half, i, k, j],
            ctx=me.across[order[j]],
        )

    def pair_copy(half, j):
        order = me.orders[half]
        src = pair_held.at[
            me.at(order[j + 1 :], other=order[j]) + (slice(None), column_half(pair_held, half))
        ]
        return remote(
            src, pair_in[2 * j + half], pps.at[half, j], ppr.at[half, j], ctx=me.across[order[j]]
        )

    def pair_add(place, source, local, cols):
        where = place + (slice(None), cols)
        total = pair_held[where].astype(jnp.float32) + source[local].astype(jnp.float32)
        pair_held[where] = total.astype(pair_held.dtype)

    def pair_stage(j):
        if j == 0:
            pair_load.wait()
            pair_core_copy.wait_recv()
            for place, local in chips_of(range(bits)):
                pair_add(place, pair_core, local, slice(None))
        else:
            for half in (0, 1):
                pair_copy(half, j - 1).wait_recv()
                for place, local in chips_of(me.orders[half][j:]):
                    pair_add(place, pair_in[2 * (j - 1) + half], local, column_half(pair_held, half))
        if j < bits:
            for half in (0, 1):
                pair_copy(half, j).start()

    tokens, weight, raw, grad_query, grad_resid = back_v
    query_width = QUERY_HEADS * HEAD_SIZE
    key_width = KEY_VALUE_HEADS * HEAD_SIZE
    own = pl.ds(0, rows)

    def head_back(cols, which, grad):
        grad = turn(grad, cosines[...], sines[...], -1.0)
        value = raw[:, cols]
        scale = lax.rsqrt(head_means(value * value) + EPSILON)
        scaled = grad * qk_gain[which : which + 1, :]
        mean = head_means(scaled * value)
        result = scale * (scaled - value * scale * scale * mean)
        projected_v[own, cols] = result.astype(jnp.bfloat16)
        return jnp.sum(grad * value * scale, axis=0, keepdims=True)

    def heads_stage():
        for load in back_loads:
            load.wait()
        sums = [jnp.zeros((1, LANES), jnp.float32)] * 2
        for j in range(0, query_width, LANES):
            cols = pl.ds(j, LANES)
            sums[0] = sums[0] + head_back(cols, 0, grad_query[:, cols] * HEAD_SIZE**-0.5)
        here = me.at()
        for j in range(0, key_width, LANES):
            first = pair_held[here + (slice(None), pl.ds(2 * j, LANES))].astype(jnp.float32)
            second = pair_held[here + (slice(None), pl.ds(2 * j + LANES, LANES))].astype(
                jnp.float32
            )
            low = low_lanes(first.shape)
            key = jnp.where(low, first, pltpu.roll(second, HEAD_SIZE, 1))
            value = jnp.where(low, pltpu.roll(first, HEAD_SIZE, 1), second)
            sums[1] = sums[1] + head_back(pl.ds(query_width + j, LANES), 1, key)
            projected_v[own, pl.ds(query_width + key_width + j, LANES)] = value.astype(jnp.bfloat16)
        both = [total + pltpu.roll(total, HEAD_SIZE, 1) for total in sums]
        small_sum[0, pl.ds(2 * gain_rows, 1), :] = jnp.where(
            low_lanes(both[0].shape), both[0], both[1]
        )
        right_copy(rights_count).start()

    gain_rows = gain.shape[1] // LANES
    width = gain.shape[1]
    inverse_mean = []

    def matmul_stage():
        inverse = row_inverse(tokens, rows)
        mean = jnp.zeros((rows, 1), jnp.float32)
        for j in range(0, width, CHUNK):
            cols = pl.ds(j, CHUNK)
            grad = dot_last(projected_v[own, :], weight[cols, :])
            grads[:, cols] = grad
            value = tokens[:, cols].astype(jnp.float32)
            mean = mean + jnp.sum(grad * gain[:, cols] * value, axis=1, keepdims=True)
        inverse_mean.extend([inverse, mean * (1.0 / width) * inverse * inverse])

    def norm_stage():
        inverse, mean = inverse_mean
        for j in range(0, width, CHUNK):
            cols = pl.ds(j, CHUNK)
            grad = grads[:, cols]
            value = tokens[:, cols].astype(jnp.float32)
            part = jnp.sum(grad * value * inverse, axis=0, keepdims=True)
            for c in range(0, CHUNK, LANES):
                small_sum[0, pl.ds((j + c) // LANES, 1), :] = part[:, c : c + LANES]
            grad_resid[:, cols] = grad_resid[:, cols] + inverse * (
                grad * gain[:, cols] - value * mean
            )
        tokens_grad_store.start()

    tokens_grad_store = pltpu.make_async_copy(grad_resid, tokens_grad, grad_sem)

    def chips_of(free):
        places, local = [()], [()]
        for b in reversed(range(bits)):
            if b in free:
                places = [t + (v,) for t in places for v in (0, 1)]
                local = [t + (v,) for t in local for v in (0, 1)]
            else:
                places = [t + (me.bit[b],) for t in places]
        return list(zip(places, local))

    def add(i, k, half, j):
        free = me.orders[half][j + 1 :]
        rows, width = held[i].shape[-2], held[i].shape[-1] // 2
        step = min(rows, 32)
        cols = pl.ds(half * width, width)
        for place, local in chips_of(free):

            def body(t, carry, place=place, local=local):
                at = pl.ds(pl.multiple_of(t * step, step), step)
                where = (target(k),) + place + (at, cols)
                total = held[i][where].astype(jnp.float32) + ins[i][j][half][
                    (k,) + local + (at,)
                ].astype(jnp.float32)
                held[i][where] = total.astype(held[i].dtype)
                return carry

            lax.fori_loop(0, rows // step, body, 0)

    def line_copy(i, k):
        return remote(
            held[i].at[(target(k),) + me.at()],
            line_in[i].at[k],
            ls.at[i, k],
            lr.at[i, k],
            fsdp=target(k),
        )

    def stage(i, k, j):
        if j == 0:
            form(i, k)
        else:
            send(i, k, j - 1)

    def send(i, k, j):
        if j > 0:
            for half in (0, 1):
                plane_copy(i, k, half, j - 1).wait_recv()
                add(i, k, half, j - 1)
        if j < bits:
            for half in (0, 1):
                plane_copy(i, k, half, j).start()
        elif k != 0:
            line_copy(i, k).start()

    def own_copy(i):
        return pltpu.make_async_copy(final[i], outs[i].at[(me.core,) + me.at()], own_sem.at[i])

    def gather_copy(i, half, j):
        order = me.orders[half]
        cols = column_half(final[i], half)
        dst = outs[i].at[(me.core,) + me.at(order[:j]) + (slice(None), cols)]
        src = final[i].at[:, cols] if j == 0 else dst
        return remote(
            src, dst, gs.at[half, i, j], gr.at[half, i, j], ctx=me.across[order[j]]
        )

    def core_copy(i):
        ref = outs[i].at[me.core]
        return remote(ref, ref, cs.at[i], cr.at[i], ctx=me.partner)

    def total(i):
        for k in range(1, nf):
            line_copy(i, k).wait_recv()
        rows = final[i].shape[0]
        step = min(rows, 32)

        def body(t, carry):
            at = pl.ds(pl.multiple_of(t * step, step), step)
            value = held[i][(z,) + me.at() + (at,)].astype(jnp.float32)
            for k in range(1, nf):
                value = value + line_in[i][k, at].astype(jnp.float32)
            final[i][at] = value.astype(final[i].dtype)
            return carry

        lax.fori_loop(0, rows // step, body, 0)
        own_copy(i).start()

    def gather_stage(i, j):
        if j == 0:
            own_copy(i).wait()
        else:
            for half in (0, 1):
                gather_copy(i, half, j - 1).wait_recv()
        if j < bits:
            for half in (0, 1):
                gather_copy(i, half, j).start()
        else:
            core_copy(i).start()

    across = [me.partner] + me.across

    def small_copy(s):
        return remote(small_sum.at[s], small_in.at[s], ss.at[s], sr.at[s], ctx=across[s])

    def small_line_copy(k):
        return remote(
            small_sum.at[bits + 1], small_line.at[z], sls.at[k], slr.at[k], fsdp=target(k)
        )

    def small_stage(s):
        if s > 0:
            small_copy(s - 1).wait_recv()
            small_sum[s] = small_sum[s - 1] + small_in[s - 1]
        if s <= bits:
            small_copy(s).start()
        else:
            for k in range(1, nf):
                small_line_copy(k).start()
            small_line[z] = small_sum[s]

    small_sum[0] = jnp.zeros(small_sum.shape[1:], jnp.float32)
    for r in range(gain_rows):
        small_sum[0, pl.ds(gain_rows + r, 1), :] = ffn_gain_part[:, r * LANES : (r + 1) * LANES]
    jobs = []
    for i in range(count):
        for k in list(range(1, nf)) + [0]:
            job = [functools.partial(stage, i, k, j) for j in range(bits + 2)]
            if k == 0:
                job += [functools.partial(total, i)]
                job += [functools.partial(gather_stage, i, j) for j in range(bits + 1)]
                job += [core_copy(i).wait_recv]
            jobs.append(job)
    back_job = [functools.partial(pair_stage, j) for j in range(bits + 1)]
    back_job += [heads_stage, matmul_stage, norm_stage]
    back_job += [functools.partial(small_stage, s) for s in range(bits + 2)]
    run_ticks(jobs[:1] + [back_job] + jobs[1:])
    for k in range(1, nf):
        small_line_copy(k).wait_recv()
    value = small_line[0]
    for k in range(1, nf):
        value = value + small_line[k]
    small_out[...] = value
    for s in range(bits + 1):
        small_copy(s).wait_send()
    for k in range(1, nf):
        small_line_copy(k).wait_send()
    for i in range(count):
        for k in range(nf):
            for half in (0, 1):
                for j in range(bits):
                    plane_copy(i, k, half, j).wait_send()
            if k:
                line_copy(i, k).wait_send()
        for half in (0, 1):
            for j in range(bits):
                gather_copy(i, half, j).wait_send()
        core_copy(i).wait_send()
    for side, n in order + [("right", rights_count)]:
        (left_copy if side == "left" else right_copy)(n).wait_send()
    pair_core_copy.wait_send()
    for half in (0, 1):
        for j in range(bits):
            pair_copy(half, j).wait_send()
    tokens_grad_store.wait()


BACK_LOADS = 5


def reduce_gradients(nf, nc, pairs, lefts, rights, grad_pair, back, ffn_gain_part):
    _, bits = plane_shape(nc)
    rows = rights[0].shape[0]
    count = len(pairs)
    views = [a.reshape(nf, 2, a.shape[0] // (2 * nf), rows) for a in lefts]
    widths = [b.shape[1] for b in rights] + [back[1].shape[1]]
    pieces = [(lefts[a].shape[0] // (nf * nc), widths[b]) for a, b in pairs]
    pair_rows, pair_width = grad_pair.shape[0] // nc, grad_pair.shape[1]
    pair_view = grad_pair.reshape((2,) * (bits + 1) + (pair_rows, pair_width))
    gain_rows = 2 * ffn_gain_part.shape[1] // LANES + 1
    small = jax.ShapeDtypeStruct((gain_rows + -gain_rows % 8, LANES), jnp.float32)
    outs = pl.pallas_call(
        functools.partial(reduce_kernel, nf, nc, pairs, len(lefts), len(rights)),
        out_shape=[
            jax.ShapeDtypeStruct((2,) * (bits + 1) + piece, jnp.bfloat16) for piece in pieces
        ]
        + [jax.ShapeDtypeStruct(back[4].shape, jnp.float32), small],
        in_specs=[HBM_SPEC] * (len(lefts) + len(rights) + 1 + BACK_LOADS) + [VMEM_SPEC] * 5,
        out_specs=[HBM_SPEC] * (count + 1) + [VMEM_SPEC],
        scratch_shapes=[
            pltpu.VMEM((nf, v.shape[2], 2 * rows), jnp.bfloat16) for v in views
        ]
        + [pltpu.VMEM((2 * rows, n), jnp.bfloat16) for n in widths]
        + [pltpu.VMEM((nf,) + (2,) * bits + piece, jnp.bfloat16) for piece in pieces]
        + [
            pltpu.VMEM((nf,) + (2,) * (bits - 1 - j) + (r, width // 2), jnp.bfloat16)
            for r, width in pieces
            for j in range(bits)
            for _ in (0, 1)
        ]
        + [pltpu.VMEM((nf,) + piece, jnp.bfloat16) for piece in pieces]
        + [pltpu.VMEM(piece, jnp.bfloat16) for piece in pieces]
        + [
            pltpu.VMEM((bits + 2,) + small.shape, jnp.float32),
            pltpu.VMEM((bits + 1,) + small.shape, jnp.float32),
            pltpu.VMEM((nf,) + small.shape, jnp.float32),
        ]
        + [pltpu.VMEM((2,) * bits + (pair_rows, pair_width), jnp.bfloat16)] * 2
        + [
            pltpu.VMEM((2,) * (bits - 1 - j) + (pair_rows, pair_width // 2), jnp.bfloat16)
            for j in range(bits)
            for _ in (0, 1)
        ]
        + [pltpu.VMEM(v.shape, v.dtype) for v in back[:BACK_LOADS]]
        + [pltpu.VMEM(back[4].shape, jnp.float32)]
        + [DMA((BACK_LOADS,)), DMA, DMA, DMA, DMA, DMA((2, bits)), DMA((2, bits))]
        + [DMA((len(lefts),))] * 3
        + [DMA((len(widths),))] * 3
        + [DMA((2, count, nf, bits))] * 2
        + [DMA((count, nf))] * 2
        + [DMA((2, count, bits))] * 2
        + [DMA((count,))] * 2
        + [DMA((count,))]
        + [DMA((bits + 1,))] * 2
        + [DMA((nf,))] * 2,
        compiler_params=pltpu.CompilerParams(
            collective_id=2, has_side_effects=True, vmem_limit_bytes=VMEM_LIMIT
        ),
        name="reduce_gradients",
    )(*views, *rights, pair_view, *back, ffn_gain_part)
    return [
        o.reshape(r * nc, width) for o, (r, width) in zip(outs, pieces)
    ], outs[count], outs[count + 1]


LANES = 128
GROUP = QUERY_HEADS // KEY_VALUE_HEADS
SMEM_SPEC = pl.BlockSpec(memory_space=pltpu.SMEM)


def low_lanes(shape):
    return lax.broadcasted_iota(jnp.int32, shape, len(shape) - 1) % LANES < HEAD_SIZE


def stack_heads(ref, row, group, length, high):
    tiles = []
    for pair in range(GROUP // 2):
        cols = pl.ds((group * GROUP // 2 + pair) * LANES, LANES)
        tile = ref[pl.ds(row, length), cols].astype(jnp.float32)
        turned = pltpu.roll(tile, HEAD_SIZE, 1)
        low = low_lanes(tile.shape)
        if high:
            tiles += [jnp.where(low, 0.0, turned), jnp.where(low, 0.0, tile)]
        else:
            tiles += [jnp.where(low, tile, 0.0), jnp.where(low, turned, 0.0)]
    return jnp.concatenate(tiles, axis=0)


def unstack_heads(ref, row, group, length, value, high):
    for pair in range(GROUP // 2):
        cols = pl.ds((group * GROUP // 2 + pair) * LANES, LANES)
        first = value[2 * pair * length : (2 * pair + 1) * length]
        second = value[(2 * pair + 1) * length : (2 * pair + 2) * length]
        low = low_lanes(first.shape)
        if high:
            tile = jnp.where(low, pltpu.roll(first, HEAD_SIZE, 1), second)
        else:
            tile = jnp.where(low, first, pltpu.roll(second, HEAD_SIZE, 1))
        ref[pl.ds(row, length), cols] = tile.astype(ref.dtype)


def query_span(rank, order, starts, stored_of, which, length):
    block = order[2 * rank + which]
    first = jnp.int32(0)
    place = block * length + lax.broadcasted_iota(jnp.int32, (1, length), 1)
    begin = jnp.zeros((1, length), jnp.int32)
    for d in range(starts.shape[1]):
        first = jnp.where(starts[0, d] <= block * length, starts[0, d], first)
        begin = jnp.where(starts[0, d] <= place, starts[0, d], begin)
    place = jnp.concatenate([place] * GROUP, axis=1)
    begin = jnp.concatenate([begin] * GROUP, axis=1)
    return block, first // length, place, begin


def invert_order(order, stored_of):
    for s in range(order.shape[0]):
        stored_of[order[s]] = s


def key_rows(stored_of, block, length, blocks):
    second = stored_of[jnp.minimum(block + 1, blocks - 1)]
    return [
        pl.ds(pl.multiple_of(s * length, length), length) for s in (stored_of[block], second)
    ]


def allowed_keys(block, place, begin, length):
    key = block * length + lax.broadcasted_iota(jnp.int32, (2 * length, place.shape[1]), 0)
    return (key >= begin) & (key <= place)


def dot_last(left, right):
    return lax.dot_general(
        left, right, (((1,), (1,)), ((), ())), preferred_element_type=jnp.float32
    )


def dot_plain(left, right):
    return lax.dot_general(
        left, right, (((1,), (0,)), ((), ())), preferred_element_type=jnp.float32
    )


def attend_kernel(rank, order, starts, query, pair, attended, exact, log_sum, stored_of, acc, queries):
    length = query.shape[0] // 2
    blocks = order.shape[0]
    invert_order(order, stored_of)

    def one_block(which, carry):
        row = pl.multiple_of(which * length, length)
        block, first, place, begin = query_span(rank[0], order, starts, stored_of, which, length)
        for g in range(KEY_VALUE_HEADS):
            queries[g] = stack_heads(query, row, g, length, False).astype(jnp.bfloat16)
        acc[...] = jnp.zeros_like(acc)

        def step(t, carry):
            key_block = first + 2 * t
            rows = key_rows(stored_of, key_block, length, blocks)
            allowed = allowed_keys(key_block, place, begin, length)
            for g in range(KEY_VALUE_HEADS):
                cols = pl.ds(g * LANES, LANES)
                keys = jnp.concatenate([pair[r, cols] for r in rows], axis=0)
                scores = dot_last(keys, queries[g])
                weights = jnp.where(allowed, jnp.exp(scores), 0.0).astype(jnp.bfloat16)
                ones = jnp.where(low_lanes(keys.shape), 1.0, keys.astype(jnp.float32))
                acc[g] += dot_plain(ones.T.astype(jnp.bfloat16), weights)
            return carry

        lax.fori_loop(0, (block - first + 2) // 2, step, 0)
        for g in range(KEY_VALUE_HEADS):
            total = acc[g]
            sums = total[0:1]
            log_sum[which, g] = jnp.broadcast_to(jnp.log(sums), log_sum.shape[2:])
            value = (total / sums).T
            unstack_heads(attended, row, g, length, value, True)
            unstack_heads(exact, row, g, length, value, True)
        return carry

    lax.fori_loop(0, 2, one_block, 0)


def attend(rank, order, starts, query, pair):
    rows = query.shape[0]
    wide = GROUP * (rows // 2)
    return pl.pallas_call(
        attend_kernel,
        out_shape=[
            jax.ShapeDtypeStruct(query.shape, jnp.bfloat16),
            jax.ShapeDtypeStruct(query.shape, jnp.float32),
            jax.ShapeDtypeStruct((2, KEY_VALUE_HEADS, 8, wide), jnp.float32),
        ],
        in_specs=[SMEM_SPEC] * 3 + [VMEM_SPEC] * 2,
        out_specs=[VMEM_SPEC] * 3,
        scratch_shapes=[
            pltpu.SMEM((order.shape[0],), jnp.int32),
            pltpu.VMEM((KEY_VALUE_HEADS, LANES, wide), jnp.float32),
            pltpu.VMEM((KEY_VALUE_HEADS, wide, LANES), jnp.bfloat16),
        ],
        name="attend",
    )(rank, order, starts, query, pair)


def attend_back_kernel(
    rank, order, starts, query, pair, grad, exact, log_sum, grad_query, grad_pair,
    stored_of, total, acc, queries, grads, delta,
):
    length = query.shape[0] // 2
    blocks = order.shape[0]
    invert_order(order, stored_of)
    total[...] = jnp.zeros_like(total)

    def one_block(which, carry):
        row = pl.multiple_of(which * length, length)
        block, first, place, begin = query_span(rank[0], order, starts, stored_of, which, length)
        for g in range(KEY_VALUE_HEADS):
            queries[g] = stack_heads(query, row, g, length, False).astype(jnp.bfloat16)
            upper = stack_heads(grad, row, g, length, True)
            grads[g] = upper.astype(jnp.bfloat16)
            product = upper * stack_heads(exact, row, g, length, True)
            delta[g] = jnp.broadcast_to(
                jnp.sum(product.T, axis=0, keepdims=True), delta.shape[1:]
            )
        acc[...] = jnp.zeros_like(acc)

        def step(t, carry):
            key_block = first + 2 * t
            rows = key_rows(stored_of, key_block, length, blocks)
            allowed = allowed_keys(key_block, place, begin, length)
            for g in range(KEY_VALUE_HEADS):
                cols = pl.ds(g * LANES, LANES)
                keys = jnp.concatenate([pair[r, cols] for r in rows], axis=0)
                scores = dot_last(keys, queries[g])
                probs = jnp.where(allowed, jnp.exp(scores - log_sum[which, g, 0:1]), 0.0)
                grad_probs = dot_last(keys, grads[g])
                grad_scores = (probs * (grad_probs - delta[g, 0:1])).astype(jnp.bfloat16)
                turned = keys.astype(jnp.float32).T.astype(jnp.bfloat16)
                acc[g] += dot_plain(turned, grad_scores)
                both = dot_plain(grad_scores, queries[g]) + dot_plain(
                    probs.astype(jnp.bfloat16), grads[g]
                )
                total[rows[0], cols] += both[:length]
                total[rows[1], cols] += both[length:]
            return carry

        lax.fori_loop(0, (block - first + 2) // 2, step, 0)
        for g in range(KEY_VALUE_HEADS):
            unstack_heads(grad_query, row, g, length, acc[g].T, False)
        return carry

    lax.fori_loop(0, 2, one_block, 0)

    def finish(t, carry):
        at = pl.ds(pl.multiple_of(t * length, length), length)
        grad_pair[at, :] = total[at, :].astype(grad_pair.dtype)
        return carry

    lax.fori_loop(0, blocks, finish, 0)


def attend_back(rank, order, starts, query, pair, grad, exact, log_sum):
    rows = query.shape[0]
    wide = GROUP * (rows // 2)
    return pl.pallas_call(
        attend_back_kernel,
        out_shape=[
            jax.ShapeDtypeStruct(query.shape, jnp.float32),
            jax.ShapeDtypeStruct(pair.shape, jnp.bfloat16),
        ],
        in_specs=[SMEM_SPEC] * 3 + [VMEM_SPEC] * 5,
        out_specs=[VMEM_SPEC] * 2,
        scratch_shapes=[
            pltpu.SMEM((order.shape[0],), jnp.int32),
            pltpu.VMEM(pair.shape, jnp.float32),
            pltpu.VMEM((KEY_VALUE_HEADS, LANES, wide), jnp.float32),
            pltpu.VMEM((KEY_VALUE_HEADS, wide, LANES), jnp.bfloat16),
            pltpu.VMEM((KEY_VALUE_HEADS, wide, LANES), jnp.bfloat16),
            pltpu.VMEM((KEY_VALUE_HEADS, 8, wide), jnp.float32),
        ],
        name="attend_back",
    )(rank, order, starts, query, pair, grad, exact, log_sum)


CHUNK = 256


def head_means(values):
    shape = (LANES, LANES)
    same = (
        lax.broadcasted_iota(jnp.int32, shape, 0) // HEAD_SIZE
        == lax.broadcasted_iota(jnp.int32, shape, 1) // HEAD_SIZE
    )
    ones = jnp.where(same, 1.0, 0.0).astype(jnp.bfloat16)
    high = values.astype(jnp.bfloat16)
    low = (values - high.astype(jnp.float32)).astype(jnp.bfloat16)
    return (dot_plain(high, ones) + dot_plain(low, ones)) * (1.0 / HEAD_SIZE)


def first_quarter(shape):
    return lax.broadcasted_iota(jnp.int32, shape, len(shape) - 1) % HEAD_SIZE < HEAD_SIZE // 2


def turn(values, cosines, sines, sign):
    half = HEAD_SIZE // 2
    ahead = pltpu.roll(values, LANES - half, 1)
    behind = pltpu.roll(values, half, 1)
    other = jnp.where(first_quarter(values.shape), -ahead, behind)
    return values * cosines + sign * other * sines


def row_inverse(ref, rows):
    total = jnp.zeros((rows, 1), jnp.float32)
    width = ref.shape[1]
    for j in range(0, width, CHUNK):
        value = ref[:, j : j + CHUNK].astype(jnp.float32)
        total = total + jnp.sum(value * value, axis=1, keepdims=True)
    return lax.rsqrt(total * (1.0 / width) + EPSILON)


def project_kernel(
    rank, order, starts, tokens, weight, gain, qk_gain, frequency,
    normed_turned, raw, query, pair, cosines, sines,
    normed,
):
    rows = tokens.shape[0]
    length = rows // 2
    for which in (0, 1):
        block = order[2 * rank[0] + which]
        place = block * length + lax.broadcasted_iota(jnp.int32, (length, LANES), 0)
        begin = jnp.zeros((length, LANES), jnp.int32)
        for d in range(starts.shape[1]):
            begin = jnp.where(starts[0, d] <= place, starts[0, d], begin)
        angle = (place - begin).astype(jnp.float32) * frequency[...]
        at = pl.ds(which * length, length)
        cosines[at, :] = jnp.cos(angle)
        sines[at, :] = jnp.sin(angle)
    inverse = row_inverse(tokens, rows)
    for j in range(0, tokens.shape[1], CHUNK):
        cols = pl.ds(j, CHUNK)
        value = tokens[:, cols].astype(jnp.float32) * inverse * gain[:, cols]
        normed[:, cols] = value.astype(jnp.bfloat16)
        normed_turned[cols, :] = value.T.astype(jnp.bfloat16)
    query_width = QUERY_HEADS * HEAD_SIZE
    key_width = KEY_VALUE_HEADS * HEAD_SIZE

    def head_turn(cols, which):
        value = raw[:, cols]
        scale = lax.rsqrt(head_means(value * value) + EPSILON)
        return turn(value * scale * qk_gain[which : which + 1, :], cosines[...], sines[...], 1.0)

    for j in range(0, weight.shape[1], CHUNK):
        raw[:, j : j + CHUNK] = dot_plain(normed[...], weight[:, j : j + CHUNK])
    for j in range(0, query_width, LANES):
        cols = pl.ds(j, LANES)
        query[:, cols] = (head_turn(cols, 0) * HEAD_SIZE**-0.5).astype(jnp.bfloat16)
    for j in range(0, key_width, LANES):
        key = head_turn(pl.ds(query_width + j, LANES), 1)
        value = raw[:, query_width + key_width + j : query_width + key_width + j + LANES]
        low = low_lanes(key.shape)
        first = jnp.where(low, key, pltpu.roll(value, HEAD_SIZE, 1))
        second = jnp.where(low, pltpu.roll(key, HEAD_SIZE, 1), value)
        pair[:, 2 * j : 2 * j + LANES] = first.astype(jnp.bfloat16)
        pair[:, 2 * j + LANES : 2 * j + 2 * LANES] = second.astype(jnp.bfloat16)


def project(rank, order, starts, tokens, weight, gain, qk_gain, frequency):
    rows, width = tokens.shape
    shape = jax.ShapeDtypeStruct
    return pl.pallas_call(
        project_kernel,
        out_shape=[
            shape((width, rows), jnp.bfloat16),
            shape((rows, weight.shape[1]), jnp.float32),
            shape((rows, QUERY_HEADS * HEAD_SIZE), jnp.bfloat16),
            shape((rows, 2 * KEY_VALUE_HEADS * HEAD_SIZE), jnp.bfloat16),
            shape((rows, LANES), jnp.float32),
            shape((rows, LANES), jnp.float32),
        ],
        in_specs=[SMEM_SPEC] * 3 + [VMEM_SPEC] * 5,
        out_specs=[VMEM_SPEC] * 6,
        scratch_shapes=[pltpu.VMEM((rows, width), jnp.bfloat16)],
        name="project",
    )(rank, order, starts, tokens, weight, gain, qk_gain, frequency)


def feed_kernel(
    tokens, cotangent, attended, gain, w_out, w_gate, w_up, w_down,
    mixed, normed_turned, hidden_turned, attended_turned, grad_gate, grad_up, grad_resid, grad_branch,
    grad_attended, gain_grad,
    out_v, gate_v, up_v, down_v, resid, normed, hidden, sems,
):
    rows, width = tokens.shape
    loads = [
        pltpu.make_async_copy(src, dst, sems.at[i])
        for i, (src, dst) in enumerate(
            ((w_out, out_v), (w_gate, gate_v), (w_up, up_v), (w_down, down_v))
        )
    ]
    for load in loads:
        load.start()
    loads[0].wait()
    for j in range(0, width, CHUNK):
        cols = pl.ds(j, CHUNK)
        resid[:, cols] = tokens[:, cols].astype(jnp.float32) + dot_plain(
            attended[...], out_v[:, cols]
        )
    inverse = row_inverse(resid, rows)
    for j in range(0, width, CHUNK):
        cols = pl.ds(j, CHUNK)
        value = resid[:, cols] * inverse * gain[:, cols]
        normed[:, cols] = value.astype(jnp.bfloat16)
        normed_turned[cols, :] = value.T.astype(jnp.bfloat16)
    for load in loads[1:]:
        load.wait()
    for j in range(0, gate_v.shape[1], CHUNK):
        cols = pl.ds(j, CHUNK)
        gate = dot_plain(normed[...], gate_v[:, cols])
        up = dot_plain(normed[...], up_v[:, cols])
        sigmoid = 1.0 / (1.0 + jnp.exp(-gate))
        inner = gate * sigmoid * up
        hidden[:, cols] = inner.astype(jnp.bfloat16)
        hidden_turned[cols, :] = inner.T.astype(jnp.bfloat16)
        grad_hidden = dot_last(cotangent[...], down_v[cols, :])
        grad_gate[:, cols] = (
            grad_hidden * up * sigmoid * (1.0 + gate * (1.0 - sigmoid))
        ).astype(jnp.bfloat16)
        grad_up[:, cols] = (grad_hidden * gate * sigmoid).astype(jnp.bfloat16)
    mean = jnp.zeros((rows, 1), jnp.float32)
    for j in range(0, width, CHUNK):
        cols = pl.ds(j, CHUNK)
        mixed[:, cols] = (resid[:, cols] + dot_plain(hidden[...], down_v[:, cols])).astype(
            jnp.bfloat16
        )
        grad = dot_last(grad_gate[...], gate_v[cols, :]) + dot_last(grad_up[...], up_v[cols, :])
        grad_resid[:, cols] = grad
        mean = mean + jnp.sum(grad * gain[:, cols] * resid[:, cols], axis=1, keepdims=True)
    mean = mean * (1.0 / width) * inverse * inverse
    for j in range(0, width, CHUNK):
        cols = pl.ds(j, CHUNK)
        grad = grad_resid[:, cols]
        value = resid[:, cols]
        gain_grad[:, cols] = jnp.sum(grad * value * inverse, axis=0, keepdims=True)
        total = cotangent[:, cols].astype(jnp.float32) + inverse * (
            grad * gain[:, cols] - value * mean
        )
        grad_resid[:, cols] = total
        grad_branch[:, cols] = total.astype(jnp.bfloat16)
    for j in range(0, attended.shape[1], CHUNK):
        cols = pl.ds(j, CHUNK)
        attended_turned[cols, :] = attended[:, cols].astype(jnp.float32).T.astype(jnp.bfloat16)
        grad_attended[:, cols] = dot_last(grad_branch[...], out_v[cols, :]).astype(jnp.bfloat16)


def feed(tokens, cotangent, attended, gain, w_out, w_gate, w_up, w_down):
    rows, width = tokens.shape
    inner = w_gate.shape[1]
    shape = jax.ShapeDtypeStruct
    low, full = jnp.bfloat16, jnp.float32
    return pl.pallas_call(
        feed_kernel,
        out_shape=[
            shape((rows, width), low),
            shape((width, rows), low),
            shape((inner, rows), low),
            shape((attended.shape[1], rows), low),
            shape((rows, inner), low),
            shape((rows, inner), low),
            shape((rows, width), full),
            shape((rows, width), low),
            shape(attended.shape, low),
            shape((1, width), full),
        ],
        in_specs=[VMEM_SPEC] * 4 + [HBM_SPEC] * 4,
        out_specs=[VMEM_SPEC] * 10,
        scratch_shapes=[pltpu.VMEM(w.shape, low) for w in (w_out, w_gate, w_up, w_down)]
        + [
            pltpu.VMEM((rows, width), full),
            pltpu.VMEM((rows, width), low),
            pltpu.VMEM((rows, inner), low),
            DMA((4,)),
        ],
        name="feed",
    )(tokens, cotangent, attended, gain, w_out, w_gate, w_up, w_down)


def pack_rows(arrays, multiple):
    flat = jnp.concatenate([a.astype(jnp.float32).reshape(-1) for a in arrays])
    size = multiple * 128
    return jnp.pad(flat, (0, -flat.shape[0] % size)).reshape(-1, 128)


def per_device(
    tokens,
    cotangent,
    doc_starts,
    deal_order,
    query_key_value_weight,
    w_out,
    w_gate,
    w_up,
    w_down,
    gain_attn,
    gain_ffn,
    gain_qk,
):
    ctx_count = lax.axis_size("ctx")
    fsdp_count = lax.axis_size("fsdp")
    ctx_rank = lax.axis_index("ctx")
    fsdp_rank = lax.axis_index("fsdp")
    model_shard = gain_attn.shape[0]
    qk_shard = gain_qk.shape[1]
    model = model_shard * fsdp_count
    gains = pack_rows([gain_attn, gain_ffn, gain_qk], 8)
    (qkv_full, out_full, gate_full, up_full, down_full), gains = gather_weights(
        fsdp_count, ctx_count, [query_key_value_weight, w_out, w_gate, w_up, w_down], gains
    )
    gains = gains.reshape(fsdp_count, -1)
    attn_gain = gains[:, :model_shard].reshape(1, model)
    ffn_gain = gains[:, model_shard : 2 * model_shard].reshape(1, model)
    qk_gain = gains[:, 2 * model_shard : 2 * model_shard + 2 * qk_shard]
    qk_gain = jnp.swapaxes(qk_gain.reshape(fsdp_count, 2, qk_shard), 0, 1).reshape(2, HEAD_SIZE)
    qk_gain = jnp.concatenate([qk_gain, qk_gain], axis=1)
    pack_in = tokens[0]
    grad_mixed = cotangent[0]
    token_rows = pack_in.shape[0]
    rank = ctx_rank.reshape(1).astype(jnp.int32)
    frequency = THETA ** (-jnp.arange(0, HEAD_SIZE // 2, dtype=jnp.float32) * 2.0 / HEAD_SIZE)
    frequency = jnp.concatenate([frequency] * (2 * LANES // HEAD_SIZE)).reshape(1, LANES)

    normed, raw, query, local_pair, cosines, sines = project(
        rank, deal_order, doc_starts, pack_in, qkv_full, attn_gain, qk_gain, frequency
    )
    pair = gather_pair(fsdp_count, ctx_count, local_pair)
    attended, exact, log_sum = attend(rank, deal_order, doc_starts, query, pair)
    (
        mixed_out,
        normed_ffn,
        hidden,
        attended_turned,
        grad_gate,
        grad_up,
        grad_resid,
        grad_branch,
        grad_attended,
        ffn_gain_part,
    ) = feed(pack_in, grad_mixed, attended, ffn_gain, out_full, gate_full, up_full, down_full)
    grad_query, grad_pair = attend_back(
        rank, deal_order, doc_starts, query, pair, grad_attended, exact, log_sum
    )
    (down_grad, gate_grad, up_grad, out_grad, qkv_grad), tokens_grad, gain_sums = reduce_gradients(
        fsdp_count,
        ctx_count,
        ((0, 0), (1, 1), (1, 2), (2, 3), (3, 4)),
        [hidden, normed_ffn, attended_turned, normed],
        [grad_mixed, grad_gate, grad_up, grad_branch],
        grad_pair,
        [
            pack_in,
            qkv_full,
            raw,
            grad_query,
            grad_resid,
            attn_gain,
            qk_gain,
            cosines,
            sines,
        ],
        ffn_gain_part,
    )
    gain_sums = gain_sums.reshape(-1)
    attn_gain_grad = lax.dynamic_slice_in_dim(gain_sums, fsdp_rank * model_shard, model_shard)
    ffn_gain_grad = lax.dynamic_slice_in_dim(
        gain_sums, model + fsdp_rank * model_shard, model_shard
    )
    qk_gain_grad = lax.dynamic_slice_in_dim(
        gain_sums[2 * model : 2 * model + 2 * HEAD_SIZE].reshape(2, HEAD_SIZE),
        fsdp_rank * qk_shard,
        qk_shard,
        axis=1,
    )
    return (
        mixed_out[None],
        tokens_grad[None],
        qkv_grad.astype(jnp.float32),
        out_grad.astype(jnp.float32),
        gate_grad.astype(jnp.float32),
        up_grad.astype(jnp.float32),
        down_grad.astype(jnp.float32),
        attn_gain_grad,
        ffn_gain_grad,
        qk_gain_grad,
    )


def solution(mesh):
    return jax.shard_map(
        per_device,
        mesh=mesh,
        in_specs=(
            P("fsdp", "ctx", None),
            P("fsdp", "ctx", None),
            P("fsdp", None),
            P(),
            P("fsdp", None),
            P("fsdp", None),
            P("fsdp", None),
            P("fsdp", None),
            P("fsdp", None),
            P("fsdp"),
            P("fsdp"),
            P(None, "fsdp"),
        ),
        out_specs=(
            P("fsdp", "ctx", None),
            P("fsdp", "ctx", None),
            P("fsdp", None),
            P("fsdp", None),
            P("fsdp", None),
            P("fsdp", None),
            P("fsdp", None),
            P("fsdp"),
            P("fsdp"),
            P(None, "fsdp"),
        ),
        check_vma=False,
    )
```

profile of v0, /device:TPU:1, one launch (start us, length us, event | category | flops | bytes accessed | tf_op | source)
XLA Modules:
  0.0 338.6 jit_solution(333550620352614509)
XLA Ops:
  0.6 0.7 reshape.127
  1.4 1.3 fusion.6.refs_5_
  2.7 101.5 %gather_weights.1 = (bf16[4,2,2,2,64,1536]{5,4,3,2,1,0:T(8,128)(2,1)}, bf16[4,2,2,2,32,2048]{5,4,3,2,1,0:T(8,128)(2,1)}, bf16[4,2,2,2,64,1024]{5,4,3,2,1,0:T(8,1...) custom-call(bf16[2,2,2,64,1536]{4,3,2,1,0:T(8,128)(2,1)} %bitcast.72, ...), custom_call_target="tpu_custom_call" | custom-call | tf_op jit(solution)/shard_map/gather_weights/pallas_call | solution.py:234
  104.2 0.8 copy.27
  105.0 0.6 copy.24
  105.6 0.1 reshape.133
  105.7 0.1 reshape.134
  105.7 0.6 pad_maximum_fusion.qk_gain.refs_15_
  106.4 0.6 maximum_bitcast_fusion.frequency
  107.0 8.3 %project.1 = (bf16[2048,256]{1,0:T(8,128)(2,1)}, f32[256,1536]{1,0:T(8,128)}, bf16[256,1024]{1,0:T(8,128)(2,1)}, bf16[256,512]{1,0:T(8,128)(2,1)}, f32[256,128]{1,0:T(8,128)}, /*index=5*/f32[256,128]{1,0:T(8,128)}) custom-call(s32[1]{0:T(128)} %bitcast.2.rank, s32[16]{0:T(128)} %order.5, s32[1,8]{1,0:T(1,128)} %starts.5, bf16[256,2048]{1,0:T(8,128)(2,1)} %bitcast.61, ...), custom_call_target="tpu_custom_call" | custom-call | tf_op jit(solution)/shard_map/project/pallas_call | solution.py:1063
  115.3 15.0 %gather_pair.1 = bf16[2,2,2,256,512]{4,3,2,1,0:T(8,128)(2,1)} custom-call(bf16[256,512]{1,0:T(8,128)(2,1)} %get-tuple-element.47.pair), custom_call_target="tpu_custom_call" | custom-call | tf_op jit(solution)/shard_map/gather_pair/pallas_call | solution.py:297
  130.3 6.8 %attend.1 = (bf16[256,1024]{1,0:T(8,128)(2,1)}, f32[256,1024]{1,0:T(8,128)}, f32[2,4,8,512]{3,2,1,0:T(8,128)}) custom-call(s32[1]{0:T(128)} %bitcast.2.rank, s32[16]{0:T(128)} %order.5, s32[1,8]{1,0:T(1,128)} %starts.5, bf16[256,1024]{1,0:T(8,128)(2,1)} %get-tuple-element.46.query, bf16[2048,512]{1,0:T(8,128)(2,1)} %bitcast.59), custom_call_target="tpu_custom_call" | custom-call | tf_op jit(solution)/shard_map/attend/pallas_call | solution.py:880
  137.1 0.6 copy.25
  137.7 17.8 %feed.1 = (bf16[256,2048]{1,0:T(8,128)(2,1)}, bf16[2048,256]{1,0:T(8,128)(2,1)}, bf16[1024,256]{1,0:T(8,128)(2,1)}, bf16[1024,256]{1,0:T(8,128)(2,1)}, bf16[256,...) custom-call(bf16[256,2048]{1,0:T(8,128)(2,1)} %bitcast.62, ...), custom_call_target="tpu_custom_call" | custom-call | tf_op jit(solution)/shard_map/feed/pallas_call | solution.py:1153
  155.5 10.8 %attend_back.1 = (f32[256,1024]{1,0:T(8,128)}, bf16[2048,512]{1,0:T(8,128)(2,1)}) custom-call(s32[1]{0:T(128)} %bitcast.2.rank, s32[16]{0:T(128)} %order.5, s32[1,8]{1,0:T(1,128)} %starts.5, bf16[256,1024]{1,0:T(8,128)(2,1)} %get-tuple-element.46.query, bf16[2048,512]{1,0:T(8,128)(2,1)} %bitcast.60, bf16[256,1024]{1,0:T(8,128)(2,1)} %get-tuple-element.61.grad, ...), custom_call_target="tpu_custom_call" | custom-call | tf_op jit(solution)/shard_map/attend_back/pallas_call | solution.py:958
  166.3 159.2 %reduce_gradients.1 = (bf16[2,2,2,32,2048]{4,3,2,1,0:T(8,128)(2,1)}, bf16[2,2,2,64,1024]{4,3,2,1,0:T(8,128)(2,1)}, bf16[2,2,2,64,1024]{4,3,2,1,0:T(8,128)(2,1)},...) custom-call(bf16[4,2,128,256]{3,2,1,0:T(8,128)(2,1)} %bitcast.79, ...), custom_call_target="tpu_custom_call" | custom-call | tf_op jit(solution)/shard_map/reduce_gradients/pallas_call | solution.py:707
  325.5 0.0 copy-start.2
  325.5 0.0 copy-start.3
  325.5 4.2 %bitcast_convert_fusion.2 = (f32[512,1024]{1,0:T(8,128)}, f32[512,1024]{1,0:T(8,128)}) fusion(bf16[2,2,2,64,1024]{4,3,2,1,0:T(8,128)(2,1)} %get-tuple-element.75, bf16[2,2,2,64,1024]{4,3,2,1,0:T(8,128)(2,1)} %get-tuple-element.74), kind=kLoop, calls=%fused_computation.2 | loop fusion | flops 1048576 | bytes 6291456 | tf_op jit(solution)/shard_map/convert_element_type | solution.py:1281
  329.7 0.0 copy-done.2
  329.7 0.0 copy-done.3
  329.7 0.0 copy-start.1
  329.7 2.7 bitcast_convert_fusion.1
  332.4 0.0 copy-done.1
  332.4 0.0 copy-start
  332.4 2.2 bitcast_convert_fusion
  334.5 1.3 fusion.7
  335.9 0.7 slice_reduce_fusion
  336.6 0.1 reshape.148
  336.6 0.6 constant_dynamic-slice_fusion
  337.3 0.0 copy-done
  337.3 1.3 copy.29
  (4 shorter events, 0.0 us)
Async XLA Ops:
  325.5 4.2 %copy-start.2 = (bf16[2,2,2,32,2048]{4,3,2,1,0:T(8,128)(2,1)S(1)}, bf16[2,2,2,32,2048]{4,3,2,1,0:T(8,128)(2,1)}, u32[]{:S(2)}) copy-start(bf16[2,2,2,32,2048]{4,3,2,1,0:T(8,128)(2,1)} %get-tuple-element.76) | copy-start | bytes 3145732
  325.5 4.2 %copy-start.3 = (bf16[2,2,2,32,2048]{4,3,2,1,0:T(8,128)(2,1)S(1)}, bf16[2,2,2,32,2048]{4,3,2,1,0:T(8,128)(2,1)}, u32[]{:S(2)}) copy-start(bf16[2,2,2,32,2048]{4,3,2,1,0:T(8,128)(2,1)} %get-tuple-element.73) | copy-start | bytes 3145732
  329.7 2.7 copy-start.1
  332.4 4.9 %copy-start = (f32[256,2048]{1,0:T(8,128)S(1)}, f32[256,2048]{1,0:T(8,128)}, u32[]{:S(2)}) copy-start(f32[256,2048]{1,0:T(8,128)} %get-tuple-element.71) | copy-start | bytes 6291460
where the time goes:
time: 338 us; the launch traced here: 339 us
  Pallas kernels  319 us (94%)
  other arithmetic  11.6 us (3%)
  local copies, waits for them, and re-layouts  6.98 us (2%)
    pallas_call x1, Pallas kernels, reduce_gradients(): pl.pallas_call(functools.partial(reduce_kernel, nf, nc, pairs, len(lefts)...  159 us
    pallas_call x1, Pallas kernels, gather_weights(): pl.pallas_call(functools.partial(gather_kernel, nf, nc, count), out_shape...  101 us
    pallas_call x1, Pallas kernels, feed(): pl.pallas_call(feed_kernel, out_shape=[shape((rows, width), low), shape((...  17.8 us
    pallas_call x1, Pallas kernels, gather_pair(): pl.pallas_call(functools.partial(gather_pair_kernel, nf, nc), out_shape=j...  15 us
    pallas_call x1, Pallas kernels, attend_back(): pl.pallas_call(attend_back_kernel, out_shape=[jax.ShapeDtypeStruct(query....  10.8 us
    pallas_call x1, Pallas kernels, project(): pl.pallas_call(project_kernel, out_shape=[shape((width, rows), jnp.bfloat...  8.32 us
    pallas_call x1, Pallas kernels, attend(): pl.pallas_call(attend_kernel, out_shape=[jax.ShapeDtypeStruct(query.shape...  6.83 us

commit v1 on v0

--- a/solution.py
+++ b/solution.py
@@ -89,20 +89,32 @@
 
 
 def gather_kernel(nf, nc, count, *refs):
-    shards, small = refs[:count], refs[count]
-    outs, small_out = refs[count + 1 : 2 * count + 1], refs[2 * count + 1]
-    stages = refs[2 * count + 2 : 3 * count + 3]
-    up_s, up_r, down_s, down_r, ps, pr, cs, cr, ss, sr, load_sem, store_sem = refs[3 * count + 3 :]
+    rest = list(refs)
+
+    def take(n):
+        return [rest.pop(0) for _ in range(n)]
+
+    shards, (small, tokens, order_of, starts, frequency) = take(count), take(5)
+    outs, (attn_gain, ffn_gain, qk_gain) = take(count), take(3)
+    normed_turned, raw, query, cosines, sines, pair = take(6)
+    weight, small_v, normed, pair_v, *stages = take(count + 3)
+    up_s, up_r, down_s, down_r, ps, pr, cs, cr, ss, sr, load_sem, store_sem = take(12)
+    pps, ppr, pcs, pcr, pair_sem = rest
+    first_out = outs[0]
+    outs = [weight] + list(outs[1:])
     me = Place(nc, nf)
     z = me.z
     loads = [
-        pltpu.make_async_copy(src, dst, load_sem.at[i])
-        for i, (src, dst) in enumerate(zip(list(shards) + [small], stages))
+        pltpu.make_async_copy(
+            shards[i], weight.at[z] if i == 0 else stages[i - 1], load_sem.at[i]
+        )
+        for i in range(count)
     ]
     stores = [
-        pltpu.make_async_copy(stages[i], dst.at[z], store_sem.at[i])
-        for i, dst in enumerate(list(outs) + [small_out])
+        pltpu.make_async_copy(stages[i - 1], outs[i].at[z], store_sem.at[i])
+        for i in range(1, count)
     ]
+    weight_store = pltpu.make_async_copy(weight, first_out, store_sem.at[0])
     for load in loads:
         load.start()
     me.barrier()
@@ -134,14 +146,18 @@
             line_copy(i, src_z, src, up).start()
 
     def small_copy(k):
-        return remote(small, small_out.at[z], ss.at[k], sr.at[k], fsdp=(z + k) % nf)
-
-    for k in range(1, nf):
-        small_copy(k).start()
-    for i in range(count):
+        return remote(small, small_v.at[z], ss.at[k], sr.at[k], fsdp=(z + k) % nf)
+
+    def own_start(i):
         mine = shards[i].at[(me.core,) + me.at()]
         line_start(i, z, mine, True, z + 1 < nf)
         line_start(i, z, mine, False, z > 0)
+
+    for k in range(1, nf):
+        small_copy(k).start()
+    for i in range(min(AHEAD, count)):
+        own_start(i)
+    small_v[z] = small[...]
 
     def line_stage(i, k):
         src_z = sources[k]
@@ -158,6 +174,8 @@
 
         line_start(i, src_z, here, True, jnp.logical_and(below, z + 1 < nf))
         line_start(i, src_z, here, False, jnp.logical_and(src_z > z, z > 0))
+        if k == nf - 1 and i + AHEAD < count:
+            own_start(i + AHEAD)
 
     def plane_copy(i, k, half, j):
         order = me.orders[half]
@@ -190,13 +208,123 @@
         + [core_copy(i, k).wait_recv]
         for i, k in order
     ]
-    for load, store in zip(loads, stores):
+    rows = tokens.shape[0]
+    length = rows // 2
+    width = tokens.shape[1]
+    query_width = QUERY_HEADS * HEAD_SIZE
+    key_width = KEY_VALUE_HEADS * HEAD_SIZE
+
+    def angle_stage():
+        for which in (0, 1):
+            block = order_of[2 * me.ctx + which]
+            place = block * length + lax.broadcasted_iota(jnp.int32, (length, LANES), 0)
+            begin = jnp.zeros((length, LANES), jnp.int32)
+            for d in range(starts.shape[1]):
+                begin = jnp.where(starts[0, d] <= place, starts[0, d], begin)
+            angle = (place - begin).astype(jnp.float32) * frequency[...]
+            at = pl.ds(which * length, length)
+            cosines[at, :] = jnp.cos(angle)
+            sines[at, :] = jnp.sin(angle)
+
+    def norm_stage():
+        for k in range(1, nf):
+            small_copy(k).wait_recv()
+        per = width // nf // LANES
+        for c in range(width // LANES):
+            cols = pl.ds(c * LANES, LANES)
+            attn_gain[:, cols] = small_v[c // per, pl.ds(c % per, 1), :]
+            ffn_gain[:, cols] = small_v[c // per, pl.ds(per + c % per, 1), :]
+        value = small_v[0, pl.ds(2 * per, 2), :]
+        for k in range(1, nf):
+            value = value + small_v[k, pl.ds(2 * per, 2), :]
+        qk_gain[...] = value
+        inverse = row_inverse(tokens, rows)
+        for j in range(0, width, CHUNK):
+            cols = pl.ds(j, CHUNK)
+            value = tokens[:, cols].astype(jnp.float32) * inverse * attn_gain[:, cols]
+            normed[:, cols] = value.astype(jnp.bfloat16)
+            normed_turned[cols, :] = value.T.astype(jnp.bfloat16)
+
+    def matmul_stage():
+        weight_store.start()
+        for j in range(0, raw.shape[1], CHUNK):
+            cols = weight[..., pl.ds(j, CHUNK)].reshape(width, CHUNK)
+            raw[:, j : j + CHUNK] = dot_plain(normed[...], cols)
+
+    def head_turn(cols, which):
+        value = raw[:, cols]
+        scale = lax.rsqrt(head_means(value * value) + EPSILON)
+        return turn(value * scale * qk_gain[which : which + 1, :], cosines[...], sines[...], 1.0)
+
+    def key_stage():
+        for j in range(0, key_width, LANES):
+            key = head_turn(pl.ds(query_width + j, LANES), 1)
+            value = raw[:, query_width + key_width + j : query_width + key_width + j + LANES]
+            low = low_lanes(key.shape)
+            first = jnp.where(low, key, pltpu.roll(value, HEAD_SIZE, 1))
+            second = jnp.where(low, pltpu.roll(key, HEAD_SIZE, 1), value)
+            pair_v[:, 2 * j : 2 * j + LANES] = first.astype(jnp.bfloat16)
+            pair_v[:, 2 * j + LANES : 2 * j + 2 * LANES] = second.astype(jnp.bfloat16)
+        for half in (0, 1):
+            pair_copy(half, 0).start()
+        pair_own_core.start()
+        pair_store.start()
+
+    def query_stage():
+        for j in range(0, query_width, LANES):
+            cols = pl.ds(j, LANES)
+            query[:, cols] = (head_turn(cols, 0) * HEAD_SIZE**-0.5).astype(jnp.bfloat16)
+
+    def pair_copy(half, j):
+        order = me.orders[half]
+        where = (slice(None), column_half(pair, half))
+        dst = pair.at[me.at(order[:j]) + (me.core,) + where]
+        src = pair_v.at[where] if j == 0 else dst
+        return remote(src, dst, pps.at[half, j], ppr.at[half, j], ctx=me.across[order[j]])
+
+    pair_own_core = remote(
+        pair_v, pair.at[me.at() + (me.core,)], pcs.at[0, 0], pcr.at[0, 0], ctx=me.partner
+    )
+    pair_store = pltpu.make_async_copy(pair_v, pair.at[me.at() + (me.core,)], pair_sem)
+
+    def pair_core_copy(half, j):
+        order = me.orders[half]
+        where = me.at(order[:j], other=order[j])
+        ref = pair.at[where + (me.core, slice(None), column_half(pair, half))]
+        return remote(ref, ref, pcs.at[half, j + 1], pcr.at[half, j + 1], ctx=me.partner)
+
+    def pair_stage(j):
+        if j == 0:
+            pair_store.wait()
+        for half in (0, 1):
+            pair_copy(half, j).wait_recv()
+        if j + 1 < me.bits:
+            for half in (0, 1):
+                pair_copy(half, j + 1).start()
+        for half in (0, 1):
+            pair_core_copy(half, j).start()
+
+    def pause():
+        pass
+
+    project_job = [norm_stage] + [pause] * me.bits
+    project_job += [matmul_stage, key_stage]
+    project_job += [functools.partial(pair_stage, j) for j in range(me.bits)]
+    angle_stage()
+    for load in loads:
         load.wait()
+    for store in stores:
         store.start()
-    run_ticks(jobs)
+    run_ticks(jobs[: nf - 1] + [project_job] + jobs[nf - 1 :])
+    query_stage()
     for k in range(1, nf):
-        small_copy(k).wait_recv()
         small_copy(k).wait_send()
+    pair_own_core.wait()
+    for j in range(me.bits):
+        for half in (0, 1):
+            pair_copy(half, j).wait_send()
+            pair_core_copy(half, j).wait()
+    weight_store.wait()
     for i in range(count):
         @pl.when(z + 1 < nf)
         def _():
@@ -226,87 +354,56 @@
         store.wait()
 
 
-def gather_weights(nf, nc, shards, small):
+AHEAD = 2
+
+
+def gather_weights(nf, nc, shards, small, tokens, order, starts, frequency):
     _, bits = plane_shape(nc)
     count = len(shards)
+    rows, width = tokens.shape
+    shape = jax.ShapeDtypeStruct
+    low, full = jnp.bfloat16, jnp.float32
+    query_width = QUERY_HEADS * HEAD_SIZE
+    pair_width = 2 * KEY_VALUE_HEADS * HEAD_SIZE
     views = [w.reshape((2,) * (1 + bits) + (w.shape[0] // nc, w.shape[1])) for w in shards]
-    arrays = views + [small]
     outs = pl.pallas_call(
         functools.partial(gather_kernel, nf, nc, count),
-        out_shape=[jax.ShapeDtypeStruct((nf,) + v.shape, v.dtype) for v in arrays],
-        in_specs=[HBM_SPEC] * (count + 1),
-        out_specs=[HBM_SPEC] * (count + 1),
-        scratch_shapes=[pltpu.VMEM(v.shape, v.dtype) for v in arrays]
+        out_shape=[shape((nf,) + v.shape, v.dtype) for v in views]
+        + [
+            shape((1, width), full),
+            shape((1, width), full),
+            shape((2, LANES), full),
+            shape((width, rows), low),
+            shape((rows, shards[0].shape[1]), full),
+            shape((rows, query_width), low),
+            shape((rows, LANES), full),
+            shape((rows, LANES), full),
+            shape((2,) * (bits + 1) + (rows, pair_width), low),
+        ],
+        in_specs=[HBM_SPEC] * count + [VMEM_SPEC] * 2 + [SMEM_SPEC] * 2 + [VMEM_SPEC],
+        out_specs=[HBM_SPEC] * count + [VMEM_SPEC] * 8 + [HBM_SPEC],
+        scratch_shapes=[
+            pltpu.VMEM((nf,) + views[0].shape, low),
+            pltpu.VMEM((nf,) + small.shape, full),
+            pltpu.VMEM((rows, width), low),
+            pltpu.VMEM((rows, pair_width), low),
+        ]
+        + [pltpu.VMEM(v.shape, v.dtype) for v in views[1:]]
         + [DMA((count, nf))] * 4
         + [DMA((2, count, nf, bits))] * 2
         + [DMA((count, nf))] * 2
         + [DMA((nf,))] * 2
-        + [DMA((count + 1,))] * 2,
-        compiler_params=pltpu.CompilerParams(collective_id=0, has_side_effects=True),
-        name="gather_weights",
-    )(*arrays)
-    return [o.reshape(nf * w.shape[0], w.shape[1]) for o, w in zip(outs, shards)], outs[count]
-
-
-def gather_pair_kernel(nf, nc, pair, out, stage, ps, pr, cs, cr, load_sem, store_sem):
-    me = Place(nc, nf)
-    load = pltpu.make_async_copy(pair, stage, load_sem)
-    load.start()
-    me.barrier(line=False)
-
-    def plane_copy(half, j):
-        order = me.orders[half]
-        where = (slice(None), column_half(out, half))
-        dst = out.at[me.at(order[:j]) + (me.core,) + where]
-        src = pair.at[where] if j == 0 else dst
-        return remote(src, dst, ps.at[half, j], pr.at[half, j], ctx=me.across[order[j]])
-
-    own_core = remote(pair, out.at[me.at() + (me.core,)], cs.at[0, 0], cr.at[0, 0], ctx=me.partner)
-
-    def core_copy(half, j):
-        order = me.orders[half]
-        ref = out.at[
-            me.at(order[:j], other=order[j]) + (me.core, slice(None), column_half(out, half))
-        ]
-        return remote(ref, ref, cs.at[half, j + 1], cr.at[half, j + 1], ctx=me.partner)
-
-    for half in (0, 1):
-        plane_copy(half, 0).start()
-    own_core.start()
-    load.wait()
-    store = pltpu.make_async_copy(stage, out.at[me.at() + (me.core,)], store_sem)
-    store.start()
-    store.wait()
-    for j in range(me.bits):
-        for half in (0, 1):
-            plane_copy(half, j).wait_recv()
-        if j + 1 < me.bits:
-            for half in (0, 1):
-                plane_copy(half, j + 1).start()
-        for half in (0, 1):
-            core_copy(half, j).start()
-    own_core.wait()
-    for j in range(me.bits):
-        for half in (0, 1):
-            plane_copy(half, j).wait_send()
-            core_copy(half, j).wait()
-
-
-def gather_pair(nf, nc, pair):
-    _, bits = plane_shape(nc)
-    out = pl.pallas_call(
-        functools.partial(gather_pair_kernel, nf, nc),
-        out_shape=jax.ShapeDtypeStruct((2,) * (bits + 1) + pair.shape, pair.dtype),
-        in_specs=[HBM_SPEC],
-        out_specs=HBM_SPEC,
-        scratch_shapes=[pltpu.VMEM(pair.shape, pair.dtype)]
+        + [DMA((count,))] * 2
         + [DMA((2, bits))] * 2
         + [DMA((2, bits + 1))] * 2
-        + [DMA, DMA],
-        compiler_params=pltpu.CompilerParams(collective_id=1, has_side_effects=True),
-        name="gather_pair",
-    )(pair)
-    return out.reshape(nc * pair.shape[0], pair.shape[1])
+        + [DMA],
+        compiler_params=pltpu.CompilerParams(
+            collective_id=0, has_side_effects=True, vmem_limit_bytes=VMEM_LIMIT
+        ),
+        name="gather_weights",
+    )(*views, small, tokens, order, starts, frequency)
+    full_weights = [o.reshape(nf * w.shape[0], w.shape[1]) for o, w in zip(outs, shards)]
+    return full_weights, outs[count:-1], outs[-1].reshape(nc * rows, pair_width)
 
 
 def reduce_kernel(nf, nc, pairs, lefts_count, rights_count, *refs):
@@ -1011,72 +1108,6 @@
     return lax.rsqrt(total * (1.0 / width) + EPSILON)
 
 
-def project_kernel(
-    rank, order, starts, tokens, weight, gain, qk_gain, frequency,
-    normed_turned, raw, query, pair, cosines, sines,
-    normed,
-):
-    rows = tokens.shape[0]
-    length = rows // 2
-    for which in (0, 1):
-        block = order[2 * rank[0] + which]
-        place = block * length + lax.broadcasted_iota(jnp.int32, (length, LANES), 0)
-        begin = jnp.zeros((length, LANES), jnp.int32)
-        for d in range(starts.shape[1]):
-            begin = jnp.where(starts[0, d] <= place, starts[0, d], begin)
-        angle = (place - begin).astype(jnp.float32) * frequency[...]
-        at = pl.ds(which * length, length)
-        cosines[at, :] = jnp.cos(angle)
-        sines[at, :] = jnp.sin(angle)
-    inverse = row_inverse(tokens, rows)
-    for j in range(0, tokens.shape[1], CHUNK):
-        cols = pl.ds(j, CHUNK)
-        value = tokens[:, cols].astype(jnp.float32) * inverse * gain[:, cols]
-        normed[:, cols] = value.astype(jnp.bfloat16)
-        normed_turned[cols, :] = value.T.astype(jnp.bfloat16)
-    query_width = QUERY_HEADS * HEAD_SIZE
-    key_width = KEY_VALUE_HEADS * HEAD_SIZE
-
-    def head_turn(cols, which):
-        value = raw[:, cols]
-        scale = lax.rsqrt(head_means(value * value) + EPSILON)
-        return turn(value * scale * qk_gain[which : which + 1, :], cosines[...], sines[...], 1.0)
-
-    for j in range(0, weight.shape[1], CHUNK):
-        raw[:, j : j + CHUNK] = dot_plain(normed[...], weight[:, j : j + CHUNK])
-    for j in range(0, query_width, LANES):
-        cols = pl.ds(j, LANES)
-        query[:, cols] = (head_turn(cols, 0) * HEAD_SIZE**-0.5).astype(jnp.bfloat16)
-    for j in range(0, key_width, LANES):
-        key = head_turn(pl.ds(query_width + j, LANES), 1)
-        value = raw[:, query_width + key_width + j : query_width + key_width + j + LANES]
-        low = low_lanes(key.shape)
-        first = jnp.where(low, key, pltpu.roll(value, HEAD_SIZE, 1))
-        second = jnp.where(low, pltpu.roll(key, HEAD_SIZE, 1), value)
-        pair[:, 2 * j : 2 * j + LANES] = first.astype(jnp.bfloat16)
-        pair[:, 2 * j + LANES : 2 * j + 2 * LANES] = second.astype(jnp.bfloat16)
-
-
-def project(rank, order, starts, tokens, weight, gain, qk_gain, frequency):
-    rows, width = tokens.shape
-    shape = jax.ShapeDtypeStruct
-    return pl.pallas_call(
-        project_kernel,
-        out_shape=[
-            shape((width, rows), jnp.bfloat16),
-            shape((rows, weight.shape[1]), jnp.float32),
-            shape((rows, QUERY_HEADS * HEAD_SIZE), jnp.bfloat16),
-            shape((rows, 2 * KEY_VALUE_HEADS * HEAD_SIZE), jnp.bfloat16),
-            shape((rows, LANES), jnp.float32),
-            shape((rows, LANES), jnp.float32),
-        ],
-        in_specs=[SMEM_SPEC] * 3 + [VMEM_SPEC] * 5,
-        out_specs=[VMEM_SPEC] * 6,
-        scratch_shapes=[pltpu.VMEM((rows, width), jnp.bfloat16)],
-        name="project",
-    )(rank, order, starts, tokens, weight, gain, qk_gain, frequency)
-
-
 def feed_kernel(
     tokens, cotangent, attended, gain, w_out, w_gate, w_up, w_down,
     mixed, normed_turned, hidden_turned, attended_turned, grad_gate, grad_up, grad_resid, grad_branch,
@@ -1204,27 +1235,28 @@
     model_shard = gain_attn.shape[0]
     qk_shard = gain_qk.shape[1]
     model = model_shard * fsdp_count
-    gains = pack_rows([gain_attn, gain_ffn, gain_qk], 8)
-    (qkv_full, out_full, gate_full, up_full, down_full), gains = gather_weights(
-        fsdp_count, ctx_count, [query_key_value_weight, w_out, w_gate, w_up, w_down], gains
-    )
-    gains = gains.reshape(fsdp_count, -1)
-    attn_gain = gains[:, :model_shard].reshape(1, model)
-    ffn_gain = gains[:, model_shard : 2 * model_shard].reshape(1, model)
-    qk_gain = gains[:, 2 * model_shard : 2 * model_shard + 2 * qk_shard]
-    qk_gain = jnp.swapaxes(qk_gain.reshape(fsdp_count, 2, qk_shard), 0, 1).reshape(2, HEAD_SIZE)
-    qk_gain = jnp.concatenate([qk_gain, qk_gain], axis=1)
     pack_in = tokens[0]
     grad_mixed = cotangent[0]
-    token_rows = pack_in.shape[0]
     rank = ctx_rank.reshape(1).astype(jnp.int32)
     frequency = THETA ** (-jnp.arange(0, HEAD_SIZE // 2, dtype=jnp.float32) * 2.0 / HEAD_SIZE)
     frequency = jnp.concatenate([frequency] * (2 * LANES // HEAD_SIZE)).reshape(1, LANES)
-
-    normed, raw, query, local_pair, cosines, sines = project(
-        rank, deal_order, doc_starts, pack_in, qkv_full, attn_gain, qk_gain, frequency
+    lane = jnp.arange(LANES) % HEAD_SIZE - fsdp_rank * qk_shard
+    own_lanes = (lane >= 0) & (lane < qk_shard)
+    qk_rows = jnp.where(own_lanes, jnp.tile(gain_qk, (1, LANES // qk_shard)), 0)
+    gains = pack_rows([gain_attn, gain_ffn, qk_rows], 8)
+    weights, (attn_gain, ffn_gain, qk_gain, normed, raw, query, cosines, sines), pair = (
+        gather_weights(
+            fsdp_count,
+            ctx_count,
+            [query_key_value_weight, w_out, w_gate, w_up, w_down],
+            gains,
+            pack_in,
+            deal_order,
+            doc_starts,
+            frequency,
+        )
     )
-    pair = gather_pair(fsdp_count, ctx_count, local_pair)
+    qkv_full, out_full, gate_full, up_full, down_full = weights
     attended, exact, log_sum = attend(rank, deal_order, doc_starts, query, pair)
     (
         mixed_out,

time: 338 us -> 315 us (0.932)
  Pallas kernels: 319 us -> 299 us
    pallas_call x2 -> x0, Pallas kernels: 23.3 us -> none  [the longest x1 15 us: gather_pair(): pl.pallas_call(functools.partial(gather_pair_kernel, nf, nc), out_shape=j...]
where the time goes in v1:
time: 315 us
  Pallas kernels  299 us (95%)
  other arithmetic  10.9 us (3%)
  local copies, waits for them, and re-layouts  4.84 us (2%)
    pallas_call x1, Pallas kernels, reduce_gradients(): pl.pallas_call(functools.partial(reduce_kernel, nf, nc, pairs, len(lefts)...  156 us
    pallas_call x1, Pallas kernels, gather_weights(): pl.pallas_call(functools.partial(gather_kernel, nf, nc, count), out_shape...  105 us
    pallas_call x1, Pallas kernels, feed(): pl.pallas_call(feed_kernel, out_shape=[shape((rows, width), low), shape((...  17.8 us
    pallas_call x1, Pallas kernels, attend_back(): pl.pallas_call(attend_back_kernel, out_shape=[jax.ShapeDtypeStruct(query....  12.8 us
    pallas_call x1, Pallas kernels, attend(): pl.pallas_call(attend_kernel, out_shape=[jax.ShapeDtypeStruct(query.shape...  7.97 us

profile of v1, /device:TPU:1, one launch (start us, length us, event | category | flops | bytes accessed | tf_op | source)
XLA Modules:
  0.0 315.4 jit_solution(7094633899594153097)
XLA Ops:
  0.7 0.7 tile.4
  1.3 0.1 tile.10
  1.4 1.3 fusion.6.refs_5_
  2.7 0.6 maximum_bitcast_fusion.refs_9_
  3.3 104.6 %gather_weights.1 = (bf16[4,2,2,2,64,1536]{5,4,3,2,1,0:T(8,128)(2,1)}, bf16[4,2,2,2,32,2048]{5,4,3,2,1,0:T(8,128)(2,1)}, bf16[4,2,2,2,64,1024]{5,4,3,2,1,0:T(8,1...) custom-call(bf16[2,2,2,64,1536]{4,3,2,1,0:T(8,128)(2,1)} %bitcast.60, ...), custom_call_target="tpu_custom_call" | custom-call | tf_op jit(solution)/shard_map/gather_weights/pallas_call | solution.py:369
  107.9 8.0 %attend.1 = (bf16[256,1024]{1,0:T(8,128)(2,1)}, f32[256,1024]{1,0:T(8,128)}, f32[2,4,8,512]{3,2,1,0:T(8,128)}) custom-call(s32[1]{0:T(128)} %bitcast.2.rank, s32[16]{0:T(128)} %order.3, s32[1,8]{1,0:T(1,128)} %starts.3, bf16[256,1024]{1,0:T(8,128)(2,1)} %get-tuple-element.46.query, bf16[2048,512]{1,0:T(8,128)(2,1)} %bitcast.49), custom_call_target="tpu_custom_call" | custom-call | tf_op jit(solution)/shard_map/attend/pallas_call | solution.py:977
  115.9 17.8 %feed.1 = (bf16[256,2048]{1,0:T(8,128)(2,1)}, bf16[2048,256]{1,0:T(8,128)(2,1)}, bf16[1024,256]{1,0:T(8,128)(2,1)}, bf16[1024,256]{1,0:T(8,128)(2,1)}, bf16[256,...) custom-call(bf16[256,2048]{1,0:T(8,128)(2,1)} %bitcast.47, ...), custom_call_target="tpu_custom_call" | custom-call | tf_op jit(solution)/shard_map/feed/pallas_call | solution.py:1184
  133.7 12.8 %attend_back.1 = (f32[256,1024]{1,0:T(8,128)}, bf16[2048,512]{1,0:T(8,128)(2,1)}) custom-call(s32[1]{0:T(128)} %bitcast.2.rank, s32[16]{0:T(128)} %order.3, s32[1,8]{1,0:T(1,128)} %starts.3, bf16[256,1024]{1,0:T(8,128)(2,1)} %get-tuple-element.46.query, bf16[2048,512]{1,0:T(8,128)(2,1)} %bitcast.50, bf16[256,1024]{1,0:T(8,128)(2,1)} %get-tuple-element.62.grad, ...), custom_call_target="tpu_custom_call" | custom-call | tf_op jit(solution)/shard_map/attend_back/pallas_call | solution.py:1055
  146.4 155.8 %reduce_gradients.1 = (bf16[2,2,2,32,2048]{4,3,2,1,0:T(8,128)(2,1)}, bf16[2,2,2,64,1024]{4,3,2,1,0:T(8,128)(2,1)}, bf16[2,2,2,64,1024]{4,3,2,1,0:T(8,128)(2,1)},...) custom-call(bf16[4,2,128,256]{3,2,1,0:T(8,128)(2,1)} %bitcast.67, ...), custom_call_target="tpu_custom_call" | custom-call | tf_op jit(solution)/shard_map/reduce_gradients/pallas_call | solution.py:804
  302.2 0.0 copy-start.2
  302.2 0.0 copy-start.3
  302.3 4.2 %bitcast_convert_fusion.2 = (f32[512,1024]{1,0:T(8,128)}, f32[512,1024]{1,0:T(8,128)}) fusion(bf16[2,2,2,64,1024]{4,3,2,1,0:T(8,128)(2,1)} %get-tuple-element.79, bf16[2,2,2,64,1024]{4,3,2,1,0:T(8,128)(2,1)} %get-tuple-element.78), kind=kLoop, calls=%fused_computation.2 | loop fusion | flops 1048576 | bytes 6291456 | tf_op jit(solution)/shard_map/convert_element_type | solution.py:1313
  306.4 0.0 copy-done.2
  306.4 0.0 copy-done.3
  306.4 0.0 copy-start.1
  306.4 2.7 bitcast_convert_fusion.1
  309.1 0.0 copy-done.1
  309.1 0.0 copy-start
  309.1 2.2 bitcast_convert_fusion
  311.3 1.3 fusion.8
  312.6 0.7 slice_reduce_fusion
  313.3 0.1 reshape.130
  313.4 0.6 constant_dynamic-slice_fusion
  314.0 0.0 copy-done
  314.0 1.3 copy.23
  (3 shorter events, 0.0 us)
Async XLA Ops:
  302.2 4.2 %copy-start.2 = (bf16[2,2,2,32,2048]{4,3,2,1,0:T(8,128)(2,1)S(1)}, bf16[2,2,2,32,2048]{4,3,2,1,0:T(8,128)(2,1)}, u32[]{:S(2)}) copy-start(bf16[2,2,2,32,2048]{4,3,2,1,0:T(8,128)(2,1)} %get-tuple-element.80) | copy-start | bytes 3145732
  302.2 4.2 %copy-start.3 = (bf16[2,2,2,32,2048]{4,3,2,1,0:T(8,128)(2,1)S(1)}, bf16[2,2,2,32,2048]{4,3,2,1,0:T(8,128)(2,1)}, u32[]{:S(2)}) copy-start(bf16[2,2,2,32,2048]{4,3,2,1,0:T(8,128)(2,1)} %get-tuple-element.77) | copy-start | bytes 3145732
  306.4 2.7 copy-start.1
  309.1 4.9 %copy-start = (f32[256,2048]{1,0:T(8,128)S(1)}, f32[256,2048]{1,0:T(8,128)}, u32[]{:S(2)}) copy-start(f32[256,2048]{1,0:T(8,128)} %get-tuple-element.75) | copy-start | bytes 6291460

commit v2 on v1

--- a/solution.py
+++ b/solution.py
@@ -354,7 +354,7 @@
         store.wait()
 
 
-AHEAD = 2
+AHEAD = 1
 
 
 def gather_weights(nf, nc, shards, small, tokens, order, starts, frequency):
@@ -855,6 +855,30 @@
     ], outs[count], outs[count + 1]
 
 
+WIDEN_STEPS = 4
+
+
+def widen_kernel(*refs):
+    count = len(refs) // 2
+    for source, target in zip(refs[:count], refs[count:]):
+        target[...] = source[...].astype(jnp.float32)
+
+
+def widen(arrays):
+    specs = [
+        pl.BlockSpec((a.shape[0] // WIDEN_STEPS, a.shape[1]), lambda t: (t, 0)) for a in arrays
+    ]
+    return pl.pallas_call(
+        widen_kernel,
+        grid=(WIDEN_STEPS,),
+        out_shape=[jax.ShapeDtypeStruct(a.shape, jnp.float32) for a in arrays],
+        in_specs=specs,
+        out_specs=specs,
+        compiler_params=pltpu.CompilerParams(vmem_limit_bytes=VMEM_LIMIT),
+        name="widen",
+    )(*arrays)
+
+
 LANES = 128
 GROUP = QUERY_HEADS // KEY_VALUE_HEADS
 SMEM_SPEC = pl.BlockSpec(memory_space=pltpu.SMEM)
@@ -1293,6 +1317,9 @@
         ],
         ffn_gain_part,
     )
+    qkv_grad, out_grad, gate_grad, up_grad, down_grad, tokens_grad = widen(
+        [qkv_grad, out_grad, gate_grad, up_grad, down_grad, tokens_grad]
+    )
     gain_sums = gain_sums.reshape(-1)
     attn_gain_grad = lax.dynamic_slice_in_dim(gain_sums, fsdp_rank * model_shard, model_shard)
     ffn_gain_grad = lax.dynamic_slice_in_dim(
@@ -1307,11 +1334,11 @@
     return (
         mixed_out[None],
         tokens_grad[None],
-        qkv_grad.astype(jnp.float32),
-        out_grad.astype(jnp.float32),
-        gate_grad.astype(jnp.float32),
-        up_grad.astype(jnp.float32),
-        down_grad.astype(jnp.float32),
+        qkv_grad,
+        out_grad,
+        gate_grad,
+        up_grad,
+        down_grad,
         attn_gain_grad,
         ffn_gain_grad,
         qk_gain_grad,

time: 315 us -> 310 us (0.984)
  other arithmetic: 10.9 us -> 1.93 us
  Pallas kernels: 299 us -> 304 us
    convert_element_type x3 -> x0, other arithmetic: 9.01 us -> none  [the longest x1 4.16 us: per_device(): up_grad.astype(jnp.float32)]
    pallas_call x0 -> x1, Pallas kernels: none -> 8.73 us  [widen(): pl.pallas_call(widen_kernel, grid=(WIDEN_STEPS,), out_shape=[jax.ShapeDty...]
    pallas_call x1, Pallas kernels: 156 us -> 150 us  [reduce_gradients(): pl.pallas_call(functools.partial(reduce_kernel, nf, nc, pairs, len(lefts)...]
where the time goes in v2:
time: 310 us
  Pallas kernels  304 us (98%)
  local copies, waits for them, and re-layouts  3.51 us (1%)
    pallas_call x1, Pallas kernels, reduce_gradients(): pl.pallas_call(functools.partial(reduce_kernel, nf, nc, pairs, len(lefts)...  150 us
    pallas_call x1, Pallas kernels, gather_weights(): pl.pallas_call(functools.partial(gather_kernel, nf, nc, count), out_shape...  104 us
    pallas_call x1, Pallas kernels, feed(): pl.pallas_call(feed_kernel, out_shape=[shape((rows, width), low), shape((...  17.8 us
    pallas_call x1, Pallas kernels, attend_back(): pl.pallas_call(attend_back_kernel, out_shape=[jax.ShapeDtypeStruct(query....  14.8 us
    pallas_call x1, Pallas kernels, attend(): pl.pallas_call(attend_kernel, out_shape=[jax.ShapeDtypeStruct(query.shape...  9.17 us
    pallas_call x1, Pallas kernels, widen(): pl.pallas_call(widen_kernel, grid=(WIDEN_STEPS,), out_shape=[jax.ShapeDty...  8.73 us

profile of v2, /device:TPU:1, one launch (start us, length us, event | category | flops | bytes accessed | tf_op | source)
XLA Modules:
  0.0 310.0 jit_solution(12648123211895390635)
XLA Ops:
  0.7 0.7 tile.4
  1.3 0.1 tile.10
  1.4 1.3 fusion.6.refs_5_
  2.7 0.6 maximum_bitcast_fusion.refs_9_
  3.3 103.6 %gather_weights.1 = (bf16[4,2,2,2,64,1536]{5,4,3,2,1,0:T(8,128)(2,1)}, bf16[4,2,2,2,32,2048]{5,4,3,2,1,0:T(8,128)(2,1)}, bf16[4,2,2,2,64,1024]{5,4,3,2,1,0:T(8,1...) custom-call(bf16[2,2,2,64,1536]{4,3,2,1,0:T(8,128)(2,1)} %bitcast.49, ...), custom_call_target="tpu_custom_call" | custom-call | tf_op jit(solution)/shard_map/gather_weights/pallas_call | solution.py:369
  107.0 9.2 %attend.1 = (bf16[256,1024]{1,0:T(8,128)(2,1)}, f32[256,1024]{1,0:T(8,128)}, f32[2,4,8,512]{3,2,1,0:T(8,128)}) custom-call(s32[1]{0:T(128)} %bitcast.2.rank, s32[16]{0:T(128)} %order.3, s32[1,8]{1,0:T(1,128)} %starts.3, bf16[256,1024]{1,0:T(8,128)(2,1)} %get-tuple-element.52.query, bf16[2048,512]{1,0:T(8,128)(2,1)} %bitcast.39), custom_call_target="tpu_custom_call" | custom-call | tf_op jit(solution)/shard_map/attend/pallas_call | solution.py:1001
  116.2 17.8 %feed.1 = (bf16[256,2048]{1,0:T(8,128)(2,1)}, bf16[2048,256]{1,0:T(8,128)(2,1)}, bf16[1024,256]{1,0:T(8,128)(2,1)}, bf16[1024,256]{1,0:T(8,128)(2,1)}, bf16[256,...) custom-call(bf16[256,2048]{1,0:T(8,128)(2,1)} %bitcast.37, ...), custom_call_target="tpu_custom_call" | custom-call | tf_op jit(solution)/shard_map/feed/pallas_call | solution.py:1208
  134.0 14.8 %attend_back.1 = (f32[256,1024]{1,0:T(8,128)}, bf16[2048,512]{1,0:T(8,128)(2,1)}) custom-call(s32[1]{0:T(128)} %bitcast.2.rank, s32[16]{0:T(128)} %order.3, s32[1,8]{1,0:T(1,128)} %starts.3, bf16[256,1024]{1,0:T(8,128)(2,1)} %get-tuple-element.52.query, bf16[2048,512]{1,0:T(8,128)(2,1)} %bitcast.40, bf16[256,1024]{1,0:T(8,128)(2,1)} %get-tuple-element.68.grad, ...), custom_call_target="tpu_custom_call" | custom-call | tf_op jit(solution)/shard_map/attend_back/pallas_call | solution.py:1079
  148.7 149.8 %reduce_gradients.1 = (bf16[2,2,2,32,2048]{4,3,2,1,0:T(8,128)(2,1)}, bf16[2,2,2,64,1024]{4,3,2,1,0:T(8,128)(2,1)}, bf16[2,2,2,64,1024]{4,3,2,1,0:T(8,128)(2,1)},...) custom-call(bf16[4,2,128,256]{3,2,1,0:T(8,128)(2,1)} %bitcast.61, ...), custom_call_target="tpu_custom_call" | custom-call | tf_op jit(solution)/shard_map/reduce_gradients/pallas_call | solution.py:804
  298.5 8.7 %widen.1 = (f32[512,1536]{1,0:T(8,128)}, f32[256,2048]{1,0:T(8,128)}, f32[512,1024]{1,0:T(8,128)}, f32[512,1024]{1,0:T(8,128)}, f32[256,2048]{1,0:T(8,128)}, /*index=5*/f32[256,2048]{1,0:T(8,128)}) custom-call(bf16[512,1536]{1,0:T(8,128)(2,1)} %bitcast.50, bf16[256,2048]{1,0:T(8,128)(2,1)} %bitcast.56, bf16[512,1024]{1,0:T(8,128)(2,1)} %bitcast.54, ...), custom_call_target="tpu_custom_call" | custom-call | tf_op jit(solution)/shard_map/widen/pallas_call | solution.py:871
  307.2 1.3 fusion.8
  308.6 0.7 slice_reduce_fusion
  309.3 0.1 reshape.135
  309.4 0.6 constant_dynamic-slice_fusion
  (3 shorter events, 0.0 us)
